TPU v7x, 32 devices: a whole 2x2x4 slice. The times are simulated.
32 devices in a mesh: dp: 16 (over z, y, core), vocab: 2 (over x).
Axes of the slice: x: 2, y: 2, z: 4, core: 2. Of those that a mesh axis runs over, the one named last changes fastest.
Arguments:
- hidden: bfloat16 [80, 512, 4096], P('dp', None, 'vocab'), may hold values from -256 to 256
- positions: int32 [80, 80], P('dp'), may hold values from 0 to 511, as said below
- labels: int32 [80, 80], P('dp'), may hold values from 0 to 127
- lse_rest: float32 [80, 80], P('dp'), may hold values from 2 to 10
- head: float32 [2, 64, 4096], P('vocab', 'dp'), may hold values from -1.5 to 1.5
- m_state: float32 [2, 64, 4096], P('vocab', 'dp'), may hold values from -80 to 80
- v_state: float32 [2, 64, 4096], P('vocab', 'dp'), may hold values from 0.5 to 20
Outputs:
- losses: float32 [80, 80], P('dp')
- new_head: float32 [2, 64, 4096], P('vocab', 'dp')
- new_m: float32 [2, 64, 4096], P('vocab', 'dp')
- new_v: float32 [2, 64, 4096], P('vocab', 'dp')
Inputs may be any that keep to these rules, and one draw needn't show every extreme that they name: The 80 positions of a sequence are distinct and ascending.
All inputs are finite; a program needn't handle non-finite values.
Results may differ from a plain program's by a relative error of at most 0.00066.
Values may be sent and summed in bfloat16 or wider, within the bound.
A program may use at most 64 MiB of HBM per device.

v0:
```python
import functools

import jax
import jax.numpy as jnp
from jax import lax
from jax.experimental import pallas as pl
from jax.experimental.pallas import tpu as pltpu
from jax.sharding import PartitionSpec as P

STEP = 100
BETA_ONE = 0.9
BETA_TWO = 0.999
ADAM_EPSILON = 1e-06
TRUST_EPSILON = 1e-06
LEARNING_RATE = 0.02

MESH = pl.DeviceIdType.MESH
CORES = 2
INNER = 2
F32 = jnp.float32
BF16 = jnp.bfloat16


def step_kernel(
    n_dp,
    hidden_ref,
    positions_hbm,
    labels_hbm,
    lse_hbm,
    head_hbm,
    m_ref,
    v_ref,
    losses_ref,
    new_head_ref,
    new_m_ref,
    new_v_ref,
    tokens,
    picked,
    pieces,
    stage,
    rows16,
    score_own,
    score_other,
    grads,
    got_core,
    send_y,
    got_y,
    send_z,
    got_z,
    send_x,
    grad_x,
    state_far,
    m_buf,
    v_buf,
    positions_ref,
    labels_ref,
    lse_ref,
    head_ref,
    update_buf,
    sums_own,
    sums,
    load_sem,
    state_sem,
    head_send,
    head_recv,
    outer_send,
    outer_recv,
    inner_send,
    inner_recv,
    core_send,
    core_recv,
    score_send,
    score_recv,
    rs_core_send,
    rs_core_recv,
    rs_y_send,
    rs_y_recv,
    rs_z_send,
    rs_z_recv,
    x_send,
    x_recv,
    sum_send,
    sum_recv,
    far_send,
    far_recv,
):
    n_outer = n_dp // (CORES * INNER)
    seqs, length, half = hidden_ref.shape
    masked = positions_ref.shape[1]
    own_rows = head_ref.shape[1]
    part = half // CORES
    dp = lax.axis_index("dp")
    v = lax.axis_index("vocab")
    c = lax.rem(dp, CORES)
    y = lax.rem(lax.div(dp, CORES), INNER)
    z = lax.div(dp, CORES * INNER)

    def at(z_to, y_to, c_to):
        return (z_to * INNER + y_to) * CORES + c_to

    def fwd(k):
        return lax.rem(z + k, n_outer)

    def back(k):
        return lax.rem(z + n_outer - k, n_outer)

    def near_last(n):
        return jnp.where(z < n_outer // 2, n_outer - n, n)

    def send(src, dst, ssem, rsem, dp_to, v_to):
        return pltpu.make_async_remote_copy(
            src_ref=src,
            dst_ref=dst,
            send_sem=ssem,
            recv_sem=rsem,
            device_id=(dp_to, v_to),
            device_id_type=MESH,
        )

    partner = at(z, y, 1 - c)
    other_y = at(z, 1 - y, c)

    def load(seq):
        return pltpu.make_async_copy(hidden_ref.at[seq], tokens.at[seq], load_sem.at[seq])

    load_positions = pltpu.make_async_copy(positions_hbm, positions_ref, state_sem.at[2])
    load_positions.start()
    load_head = pltpu.make_async_copy(head_hbm, head_ref, state_sem.at[5])
    load_head.start()
    for seq in range(seqs):
        load(seq).start()
    load_labels = pltpu.make_async_copy(labels_hbm, labels_ref, state_sem.at[3])
    load_lse = pltpu.make_async_copy(lse_hbm, lse_ref, state_sem.at[4])
    load_m = pltpu.make_async_copy(m_ref, m_buf, state_sem.at[0])
    load_v = pltpu.make_async_copy(v_ref, v_buf, state_sem.at[1])
    for copy in (load_labels, load_lse, load_m, load_v):
        copy.start()

    sent = []

    def finish():
        for low_k, high_k, copies in sent:

            @pl.loop(low_k, high_k)
            def _(k, copies=copies):
                for copy in copies(k):
                    copy.wait_send()

    barrier = pltpu.get_barrier_semaphore()

    def greet(dp_to, v_to):
        pl.semaphore_signal(barrier, inc=1, device_id=(dp_to, v_to), device_id_type=MESH)

    @pl.loop(1, n_outer)
    def _(k):
        greet(at(fwd(k), y, c), v)

    greet(other_y, v)
    greet(partner, v)
    greet(dp, 1 - v)
    greet(partner, 1 - v)
    def pick(seq):
        load(seq).wait()
        spots = positions_ref[pl.ds(seq, 1), :]
        hot = lax.broadcasted_iota(jnp.int32, (length, masked), 0) == spots
        picked[seq] = lax.dot_general(
            jnp.where(hot, 1.0, 0.0).astype(BF16),
            tokens[seq],
            (((0,), (0,)), ((), ())),
            preferred_element_type=F32,
        ).astype(BF16)

    def picks(low, high):
        @pl.loop(low, high)
        def _(seq):
            pick(seq)

    load_positions.wait()
    load_head.wait()
    pl.semaphore_wait(barrier, n_outer + 3)

    def head_half(h):
        return head_ref.at[0, :, pl.ds(pl.multiple_of(h * half, half), half)]

    slot = 2 * c + v
    head_copies = [
        send(head_half(v), pieces.at[slot], head_send.at[0], head_recv.at[slot], partner, v),
        send(head_half(1 - v), pieces.at[slot], head_send.at[1], head_recv.at[slot], dp, 1 - v),
        send(
            head_half(1 - v), pieces.at[slot], head_send.at[2], head_recv.at[slot], partner, 1 - v
        ),
    ]
    for copy in head_copies:
        copy.start()

    def state_cols(ref):
        return ref.at[0, :, pl.ds(pl.multiple_of((1 - v) * half, half), half)]

    state_copies = [
        send(state_cols(m_ref), state_far.at[0], far_send.at[0], far_recv.at[0], dp, 1 - v),
        send(state_cols(v_ref), state_far.at[1], far_send.at[1], far_recv.at[1], dp, 1 - v),
    ]
    for copy in state_copies:
        copy.start()
    sent.append((0, 1, lambda k: head_copies + state_copies))
    pieces[slot] = head_ref[0, :, pl.ds(pl.multiple_of(v * half, half), half)]
    whole_head = head_ref[0]
    weight_part = jnp.sum(whole_head * whole_head, axis=(0, 1), keepdims=True)

    picks(0, 1)
    for slot_from in (
        2 * (1 - c) + v,
        2 * c + 1 - v,
        2 * (1 - c) + 1 - v,
    ):
        send(
            head_half(0), pieces.at[slot_from], head_send.at[0], head_recv.at[slot_from], dp, 1 - v
        ).wait_recv()
    for k in range(2 * CORES):
        stage[k * own_rows : (k + 1) * own_rows, :] = pieces[k]
    rows16[z * INNER + y] = stage[...].astype(BF16)

    columns = pl.ds(pl.multiple_of(c * part, part), part)
    columns_other = pl.ds(pl.multiple_of((1 - c) * part, part), part)

    def rows_of(z_of, y_of, cols):
        return rows16.at[z_of * INNER + y_of, :, cols]

    def outer_copy(k, z_of):
        ref = rows_of(z_of, y, columns)
        return send(ref, ref, outer_send.at[k], outer_recv.at[k], at(fwd(k), y, c), v)

    def inner_copy(k, y_of):
        ref = rows_of(back(k), y_of, columns)
        return send(ref, ref, inner_send.at[k], inner_recv.at[k], other_y, v)

    def core_copy(k, y_of, index, cols):
        ref = rows_of(back(k), y_of, cols)
        return send(ref, ref, core_send.at[index], core_recv.at[index], partner, v)

    inner_copy(0, y).start()
    sent.append((1, n_outer, lambda k: (outer_copy(k, z), core_copy(k, y, k, columns))))
    sent.append(
        (0, n_outer, lambda k: (inner_copy(k, y), core_copy(k, 1 - y, n_outer + k, columns)))
    )

    @pl.loop(1, n_outer)
    def _(n):
        outer_copy(near_last(n), z).start()

    picks(1, seqs)

    @pl.loop(1, n_outer)
    def _(n):
        k = near_last(n)
        outer_copy(k, back(k)).wait_recv()
        inner_copy(k, y).start()
        core_copy(k, y, k, columns).start()

    load_labels.wait()
    load_lse.wait()

    inner_copy(0, 1 - y).wait_recv()
    core_copy(0, 1 - y, n_outer, columns).start()

    @pl.loop(1, n_outer)
    def _(n):
        k = near_last(n)
        inner_copy(k, 1 - y).wait_recv()
        core_copy(k, 1 - y, n_outer + k, columns).start()

    @pl.loop(1, n_outer)
    def _(k):
        core_copy(k, y, k, columns_other).wait_recv()

    @pl.loop(0, n_outer)
    def _(k):
        core_copy(k, 1 - y, n_outer + k, columns_other).wait_recv()

    block = n_dp * 2 * own_rows

    def score_copy(seq):
        return send(
            score_own.at[seq],
            score_other.at[seq],
            score_send.at[seq],
            score_recv.at[seq],
            dp,
            1 - v,
        )

    @pl.loop(0, seqs)
    def _(seq):
        score_own[seq] = lax.dot_general(
            picked[seq],
            rows16[...].reshape(block, half),
            (((1,), (1,)), ((), ())),
            preferred_element_type=F32,
        )
        score_copy(seq).start()

    sent.append((0, seqs, lambda seq: (score_copy(seq),)))
    grads[...] = jnp.zeros_like(grads)
    row = lax.broadcasted_iota(jnp.int32, (block, masked), 0)
    shift = own_rows.bit_length() - 1
    row_id = (
        (lax.shift_right_logical(row, shift) & 1) * (n_dp * own_rows)
        + lax.shift_right_logical(row, shift + 1) * own_rows
        + (row & (own_rows - 1))
    )

    @pl.loop(0, seqs)
    def _(seq):
        score_copy(seq).wait_recv()
        scores = jnp.transpose(score_own[seq] + score_other[seq])
        rest = lse_ref[pl.ds(seq, 1), :]
        top = jnp.maximum(jnp.max(scores, axis=0, keepdims=True), rest)
        total = jnp.exp(rest - top) + jnp.sum(jnp.exp(scores - top), axis=0, keepdims=True)
        row_lse = top + jnp.log(total)
        hits = row_id == labels_ref[pl.ds(seq, 1), :]
        target = jnp.sum(jnp.where(hits, scores, 0.0), axis=0, keepdims=True)
        losses_ref[pl.ds(seq, 1), :] = row_lse - target
        logit_grad = (jnp.exp(scores - row_lse) - jnp.where(hits, 1.0, 0.0)).astype(BF16)
        grads[...] += lax.dot_general(
            logit_grad, picked[seq], (((1,), (0,)), ((), ())), preferred_element_type=F32
        ).reshape(n_dp, 2 * own_rows, half)

    def rs_core(k, y_of):
        return send(
            grads.at[at(fwd(k), y_of, 1 - c)],
            got_core.at[k, y_of],
            rs_core_send.at[k, y_of],
            rs_core_recv.at[k, y_of],
            partner,
            v,
        )

    def rs_y(k):
        return send(send_y.at[k], got_y.at[k], rs_y_send.at[k], rs_y_recv.at[k], other_y, v)

    def rs_z(k):
        return send(
            send_z.at[k], got_z.at[k], rs_z_send.at[k], rs_z_recv.at[k], at(fwd(k), y, c), v
        )

    sent.append((0, n_outer, lambda k: (rs_core(k, 0), rs_core(k, 1), rs_y(k))))
    sent.append((1, n_outer, lambda k: (rs_z(k),)))

    def later(n):
        return lax.rem(near_last(n + 1), n_outer) * jnp.where(n == n_outer - 1, 0, 1)

    @pl.loop(0, n_outer)
    def _(n):
        rs_core(later(n), 1 - y).start()

    @pl.loop(0, n_outer)
    def _(n):
        rs_core(later(n), y).start()

    @pl.loop(0, n_outer)
    def _(n):
        k = later(n)
        rs_core(k, 1 - y).wait_recv()
        send_y[k] = grads[at(fwd(k), 1 - y, c)] + got_core[k, 1 - y]
        rs_y(k).start()

    @pl.loop(1, n_outer)
    def _(n):
        k = near_last(n)
        rs_core(k, y).wait_recv()
        rs_y(k).wait_recv()
        send_z[k] = grads[at(fwd(k), y, c)] + got_core[k, y] + got_y[k]
        rs_z(k).start()

    rs_core(0, y).wait_recv()
    rs_y(0).wait_recv()
    rows8 = grads[at(z, y, c)] + got_core[0, y] + got_y[0]
    for k in range(1, n_outer):
        rs_z(k).wait_recv()
        rows8 = rows8 + got_z[k]
    low, high = rows8[:own_rows], rows8[own_rows:]
    grad_near = jnp.where(v == 0, low, high)
    grad_far = jnp.where(v == 0, high, low)
    send_x[...] = grad_far
    x_copy = send(send_x, grad_x, x_send, x_recv, dp, 1 - v)
    x_copy.start()
    sent.append((0, 1, lambda k: (x_copy,)))
    load_m.wait()
    load_v.wait()
    for copy in state_copies:
        copy.wait_recv()

    first_fix = 1.0 - BETA_ONE**STEP
    second_fix = 1.0 - BETA_TWO**STEP

    def lamb(grad, first, second):
        first = BETA_ONE * first + (1.0 - BETA_ONE) * grad
        second = BETA_TWO * second + (1.0 - BETA_TWO) * grad * grad
        update = first / first_fix / (jnp.sqrt(second / second_fix) + ADAM_EPSILON)
        return first, second, update

    def square_sum(values):
        return jnp.sum(values * values, axis=(0, 1), keepdims=True)

    def finish_half(grad, h):
        cols = pl.ds(pl.multiple_of(h * half, half), half)
        first, second, update = lamb(grad, m_buf[0, :, cols], v_buf[0, :, cols])
        new_m_ref[0, :, cols] = first
        new_v_ref[0, :, cols] = second
        update_buf[:, cols] = update
        return update

    lane = lax.broadcasted_iota(jnp.int32, (1, 128), 1)
    _, _, update_far = lamb(grad_far, state_far[0], state_far[1])
    sums_own[1] = jnp.where(lane == 0, square_sum(update_far), 0.0)
    near = jnp.where(
        lane == 0,
        square_sum(finish_half(grad_near, v)),
        jnp.where(lane == 1, weight_part, 0.0),
    )
    sums_own[0] = near

    def sum_far(k, to, slot_of):
        return send(
            sums_own.at[1], sums.at[1, slot_of], sum_send.at[1, k], sum_recv.at[1, k], to, 1 - v
        )

    def sum_near(k, to, slot_of):
        return send(
            sums_own.at[0], sums.at[0, slot_of], sum_send.at[0, k], sum_recv.at[0, k], to, v
        )

    def to_dp(k):
        return lax.rem(dp + k, n_dp)

    def from_dp(k):
        return lax.rem(dp + n_dp - k, n_dp)

    sums[0, dp] = near

    @pl.loop(1, n_dp)
    def _(n):
        k = jnp.where(z < n_outer // 2, n_dp - n, n)
        sum_far(k, to_dp(k), dp).start()
        sum_near(k, to_dp(k), dp).start()

    sum_far(0, dp, dp).start()

    sent.append((0, n_dp, lambda k: (sum_far(k, to_dp(k), dp),)))
    sent.append((1, n_dp, lambda k: (sum_near(k, to_dp(k), dp),)))
    x_copy.wait_recv()
    finish_half(grad_x[...], 1 - v)

    @pl.loop(0, n_dp)
    def _(k):
        sum_far(k, to_dp(k), from_dp(k)).wait_recv()

    @pl.loop(1, n_dp)
    def _(k):
        sum_near(k, to_dp(k), from_dp(k)).wait_recv()

    totals = jnp.sum(jnp.sum(sums[...], axis=0), axis=0)
    update_total = jnp.sum(jnp.where(lane == 0, totals, 0.0), axis=1, keepdims=True)
    weight_total = jnp.sum(jnp.where(lane == 1, totals, 0.0), axis=1, keepdims=True)
    trust = jnp.sqrt(weight_total) / (jnp.sqrt(update_total) + TRUST_EPSILON)
    new_head_ref[0] = head_ref[0] - LEARNING_RATE * trust * update_buf[...]
    finish()


def store_kernel(*refs):
    count = (len(refs) - 1) // 2
    sems = refs[-1]
    copies = [
        pltpu.make_async_copy(refs[n], refs[count + n], sems.at[n]) for n in range(count)
    ]
    for copy in copies:
        copy.start()
    for copy in copies:
        copy.wait()


def fused_step(n_dp, hidden, positions, labels, lse_rest, head, m_state, v_state):
    seqs, length, half = hidden.shape
    masked = positions.shape[1]
    own_rows, width = head.shape[1], head.shape[2]
    n_outer = n_dp // (CORES * INNER)
    pair = 2 * own_rows
    block = n_dp * pair
    vmem = pl.BlockSpec(memory_space=pltpu.VMEM)
    anywhere = pl.BlockSpec(memory_space=pltpu.HBM)
    dma = pltpu.SemaphoreType.DMA
    state = jax.ShapeDtypeStruct(head.shape, F32)
    operands = [
        pltpu.with_memory_space_constraint(operand, pltpu.HBM)
        for operand in (hidden, positions, labels, lse_rest, head, m_state, v_state)
    ]
    results = pl.pallas_call(
        functools.partial(step_kernel, n_dp),
        out_shape=(jax.ShapeDtypeStruct(lse_rest.shape, F32), state, state, state),
        in_specs=[anywhere] * 7,
        out_specs=(vmem, vmem, vmem, vmem),
        scratch_shapes=[
            pltpu.VMEM((seqs, length, half), BF16),
            pltpu.VMEM((seqs, masked, half), BF16),
            pltpu.VMEM((2 * CORES, own_rows, half), F32),
            pltpu.VMEM((2 * CORES * own_rows, half), F32),
            pltpu.VMEM((n_dp // CORES, CORES * pair, half), BF16),
            pltpu.VMEM((seqs, masked, block), F32),
            pltpu.VMEM((seqs, masked, block), F32),
            pltpu.VMEM((n_dp, pair, half), F32),
            pltpu.VMEM((n_outer, INNER, pair, half), F32),
            pltpu.VMEM((n_outer, pair, half), F32),
            pltpu.VMEM((n_outer, pair, half), F32),
            pltpu.VMEM((n_outer, pair, half), F32),
            pltpu.VMEM((n_outer, pair, half), F32),
            pltpu.VMEM((own_rows, half), F32),
            pltpu.VMEM((own_rows, half), F32),
            pltpu.VMEM((2, own_rows, half), F32),
            pltpu.VMEM((1, own_rows, width), F32),
            pltpu.VMEM((1, own_rows, width), F32),
            pltpu.VMEM(positions.shape, jnp.int32),
            pltpu.VMEM(labels.shape, jnp.int32),
            pltpu.VMEM(lse_rest.shape, F32),
            pltpu.VMEM(head.shape, F32),
            pltpu.VMEM((own_rows, width), F32),
            pltpu.VMEM((2, 1, 128), F32),
            pltpu.VMEM((2, n_dp, 1, 128), F32),
            dma((seqs,)),
            dma((6,)),
            dma((3,)),
            dma((2 * CORES,)),
            dma((n_outer,)),
            dma((n_outer,)),
            dma((n_outer,)),
            dma((n_outer,)),
            dma((2 * n_outer,)),
            dma((2 * n_outer,)),
            dma((seqs,)),
            dma((seqs,)),
            dma((n_outer, INNER)),
            dma((n_outer, INNER)),
            dma((n_outer,)),
            dma((n_outer,)),
            dma((n_outer,)),
            dma((n_outer,)),
            dma,
            dma,
            dma((2, n_dp)),
            dma((2, n_dp)),
            dma((2,)),
            dma((2,)),
        ],
        compiler_params=pltpu.CompilerParams(
            collective_id=0, has_side_effects=True, vmem_limit_bytes=48 * 1024 * 1024
        ),
        name="fused_step",
    )(*operands)
    count = len(results)
    return pl.pallas_call(
        store_kernel,
        out_shape=tuple(jax.ShapeDtypeStruct(r.shape, r.dtype) for r in results),
        in_specs=[vmem] * count,
        out_specs=(anywhere,) * count,
        scratch_shapes=[dma((count,))],
        compiler_params=pltpu.CompilerParams(vmem_limit_bytes=4 * 1024 * 1024),
        name="store_results",
    )(*results)


def on_device(hidden, positions, labels, lse_rest, head, m_state, v_state):
    seq_here, mask_here = positions.shape
    rows_here = seq_here * mask_here
    own_rows = head.shape[1]
    model_width = head.shape[2]
    head_own = head.reshape(own_rows, model_width)
    weight_total = lax.psum(jnp.sum(head_own * head_own), "dp")
    local_rows = jnp.take_along_axis(hidden, positions[:, :, None], axis=1).reshape(
        rows_here, hidden.shape[2]
    )
    picked = lax.all_gather(local_rows, "vocab", axis=1, tiled=True)
    head_copy = head_own.astype(jnp.bfloat16)
    scores = lax.dot_general(
        picked,
        lax.all_gather(head_copy, "dp", axis=0, tiled=True),
        (((1,), (1,)), ((), ())),
        preferred_element_type=jnp.float32,
    )
    slab_width = scores.shape[1]
    offset = lax.axis_index("vocab") * slab_width
    label_local = labels.reshape(rows_here) - offset
    label_hits = label_local[:, None] == lax.iota(jnp.int32, slab_width)[None, :]
    target_part = jnp.sum(jnp.where(label_hits, scores, 0.0), axis=1)
    rest_lse = lse_rest.reshape(rows_here)
    slab_max = jnp.max(scores, axis=1)
    block_max = lax.pmax(slab_max, "vocab")
    row_top = jnp.maximum(block_max, rest_lse)
    slab_sum = jnp.sum(jnp.exp(scores - row_top[:, None]), axis=1)
    block_sum, target = lax.psum((slab_sum, target_part), "vocab")
    row_total = block_sum + jnp.exp(rest_lse - row_top)
    row_lse = row_top + jnp.log(row_total)
    losses = (row_lse - target).reshape(seq_here, mask_here)
    logit_grad = (jnp.exp(scores - row_lse[:, None]) - label_hits.astype(jnp.float32)).astype(
        jnp.bfloat16
    )
    full_grad = lax.dot_general(
        logit_grad, picked, (((0,), (0,)), ((), ())), preferred_element_type=jnp.float32
    )
    head_grad = lax.psum_scatter(full_grad, "dp", scatter_dimension=0, tiled=True)
    first_moment = BETA_ONE * m_state.reshape(own_rows, model_width) + (1.0 - BETA_ONE) * head_grad
    second_moment = (
        BETA_TWO * v_state.reshape(own_rows, model_width) + (1.0 - BETA_TWO) * head_grad * head_grad
    )
    first_fix = 1.0 - BETA_ONE**STEP
    second_fix = 1.0 - BETA_TWO**STEP
    update = first_moment / first_fix / (jnp.sqrt(second_moment / second_fix) + ADAM_EPSILON)
    update_part = jnp.sum(update * update)
    update_total = lax.psum(update_part, "dp")
    trust_ratio = jnp.sqrt(weight_total) / (jnp.sqrt(update_total) + TRUST_EPSILON)
    new_head = head_own - LEARNING_RATE * trust_ratio * update
    return (
        losses,
        new_head.reshape(head.shape),
        first_moment.reshape(head.shape),
        second_moment.reshape(head.shape),
    )


def pairwise(mesh, args):
    n_dp, n_vocab = mesh.shape["dp"], mesh.shape["vocab"]
    own_rows = args[4].shape[1] // n_dp
    power_of_two = own_rows & (own_rows - 1) == 0
    return n_vocab == 2 and n_dp % (CORES * INNER) == 0 and power_of_two


def solution(mesh):
    def step(*args):
        if pairwise(mesh, args):
            body = functools.partial(fused_step, mesh.shape["dp"])
        else:
            body = on_device
        return sharded(mesh, body)(*args)

    return step


def sharded(mesh, body):
    return jax.shard_map(
        body,
        mesh=mesh,
        in_specs=(
            P("dp", None, "vocab"),
            P("dp", None),
            P("dp", None),
            P("dp", None),
            P("vocab", "dp", None),
            P("vocab", "dp", None),
            P("vocab", "dp", None),
        ),
        out_specs=(
            P("dp", None),
            P("vocab", "dp", None),
            P("vocab", "dp", None),
            P("vocab", "dp", None),
        ),
        check_vma=False,
    )
```

profile of v0, /device:TPU:0, one launch (start us, length us, event | category | flops | bytes accessed | tf_op | source)
XLA Modules:
  0.0 44.0 jit_solution(11410232374929514745)
XLA Ops:
  0.6 42.6 %fused_step.1 = (f32[5,80]{1,0:T(8,128)S(1)}, f32[1,4,4096]{2,1,0:T(4,128)S(1)}, f32[1,4,4096]{2,1,0:T(4,128)S(1)}, f32[1,4,4096]{2,1,0:T(4,128)S(1)}) custom-call(bf16[5,512,2048]{2,1,0:T(8,128)(2,1)} %hidden_ref.1, s32[5,80]{1,0:T(8,128)} %positions_hbm.1, s32[5,80]{1,0:T(8,128)} %labels_hbm.1, f32[5,80]{1,0:T(8,128)} %lse_hbm.1, f32[1,4,4096]{2,1,0:T(4,128)} %head_hbm.1, ...), custom_call_target="tpu_custom_call" | custom-call | tf_op jit(solution)/shard_map/fused_step/pallas_call | solution.py:497
  43.2 0.7 %store_results.1 = (f32[5,80]{1,0:T(8,128)}, f32[1,4,4096]{2,1,0:T(4,128)}, f32[1,4,4096]{2,1,0:T(4,128)}, f32[1,4,4096]{2,1,0:T(4,128)}) custom-call(f32[5,80]{1,0:T(8,128)S(1)} %get-tuple-element.8.refs_0_, f32[1,4,4096]{2,1,0:T(4,128)S(1)} %get-tuple-element.9.refs_1_, f32[1,4,4096]{2,1,0:T(4,128)S(1)} %get-tuple-element.10.refs_2_, ...), custom_call_target="tpu_custom_call" | custom-call | tf_op jit(solution)/shard_map/store_results/pallas_call | solution.py:559
where the time goes:
time: 44.1 us; the launch traced here: 44 us
  Pallas kernels  43.3 us (98%)
  between operations  0.64 us (1%)
    pallas_call x1, Pallas kernels, fused_step(): pl.pallas_call(functools.partial(step_kernel, n_dp), out_shape=(jax.Shape...  42.6 us

commit v1 on v0

--- a/solution.py
+++ b/solution.py
@@ -61,27 +61,17 @@
     sums,
     load_sem,
     state_sem,
-    head_send,
+    all_sent,
     head_recv,
-    outer_send,
     outer_recv,
-    inner_send,
     inner_recv,
-    core_send,
     core_recv,
-    score_send,
     score_recv,
-    rs_core_send,
     rs_core_recv,
-    rs_y_send,
     rs_y_recv,
-    rs_z_send,
     rs_z_recv,
-    x_send,
     x_recv,
-    sum_send,
     sum_recv,
-    far_send,
     far_recv,
 ):
     n_outer = n_dp // (CORES * INNER)
@@ -179,16 +169,14 @@
     load_head.wait()
     pl.semaphore_wait(barrier, n_outer + 3)
 
-    def head_half(h):
-        return head_ref.at[0, :, pl.ds(pl.multiple_of(h * half, half), half)]
+    def head_part(v_of, c_of):
+        start = pl.multiple_of(v_of * half + c_of * part, part)
+        return head_ref.at[0, :, pl.ds(start, part)]
 
     slot = 2 * c + v
     head_copies = [
-        send(head_half(v), pieces.at[slot], head_send.at[0], head_recv.at[slot], partner, v),
-        send(head_half(1 - v), pieces.at[slot], head_send.at[1], head_recv.at[slot], dp, 1 - v),
-        send(
-            head_half(1 - v), pieces.at[slot], head_send.at[2], head_recv.at[slot], partner, 1 - v
-        ),
+        send(head_part(v_to, c_to), pieces.at[slot], all_sent, head_recv.at[slot], at(z, y, c_to), v_to)
+        for v_to, c_to in ((1 - v, c), (1 - v, 1 - c), (v, 1 - c))
     ]
     for copy in head_copies:
         copy.start()
@@ -197,13 +185,11 @@
         return ref.at[0, :, pl.ds(pl.multiple_of((1 - v) * half, half), half)]
 
     state_copies = [
-        send(state_cols(m_ref), state_far.at[0], far_send.at[0], far_recv.at[0], dp, 1 - v),
-        send(state_cols(v_ref), state_far.at[1], far_send.at[1], far_recv.at[1], dp, 1 - v),
+        send(state_cols(m_ref), state_far.at[0], all_sent, far_recv.at[0], dp, 1 - v),
+        send(state_cols(v_ref), state_far.at[1], all_sent, far_recv.at[1], dp, 1 - v),
     ]
-    for copy in state_copies:
-        copy.start()
     sent.append((0, 1, lambda k: head_copies + state_copies))
-    pieces[slot] = head_ref[0, :, pl.ds(pl.multiple_of(v * half, half), half)]
+    pieces[slot] = head_ref[0, :, pl.ds(pl.multiple_of(v * half + c * part, part), part)]
     whole_head = head_ref[0]
     weight_part = jnp.sum(whole_head * whole_head, axis=(0, 1), keepdims=True)
 
@@ -214,13 +200,12 @@
         2 * (1 - c) + 1 - v,
     ):
         send(
-            head_half(0), pieces.at[slot_from], head_send.at[0], head_recv.at[slot_from], dp, 1 - v
+            head_part(0, 0), pieces.at[slot_from], all_sent, head_recv.at[slot_from], dp, 1 - v
         ).wait_recv()
     for k in range(2 * CORES):
         stage[k * own_rows : (k + 1) * own_rows, :] = pieces[k]
-    rows16[z * INNER + y] = stage[...].astype(BF16)
-
     columns = pl.ds(pl.multiple_of(c * part, part), part)
+    rows16[z * INNER + y, :, columns] = stage[...].astype(BF16)
     columns_other = pl.ds(pl.multiple_of((1 - c) * part, part), part)
 
     def rows_of(z_of, y_of, cols):
@@ -228,20 +213,29 @@
 
     def outer_copy(k, z_of):
         ref = rows_of(z_of, y, columns)
-        return send(ref, ref, outer_send.at[k], outer_recv.at[k], at(fwd(k), y, c), v)
+        return send(ref, ref, all_sent, outer_recv.at[k], at(fwd(k), y, c), v)
 
     def inner_copy(k, y_of):
         ref = rows_of(back(k), y_of, columns)
-        return send(ref, ref, inner_send.at[k], inner_recv.at[k], other_y, v)
+        return send(ref, ref, all_sent, inner_recv.at[k], other_y, v)
 
     def core_copy(k, y_of, index, cols):
         ref = rows_of(back(k), y_of, cols)
-        return send(ref, ref, core_send.at[index], core_recv.at[index], partner, v)
+        return send(ref, ref, all_sent, core_recv.at[index], partner, v)
 
     inner_copy(0, y).start()
-    sent.append((1, n_outer, lambda k: (outer_copy(k, z), core_copy(k, y, k, columns))))
+    core_copy(0, y, 0, columns).start()
+    sent.append((1, n_outer, lambda k: (outer_copy(k, z),)))
     sent.append(
-        (0, n_outer, lambda k: (inner_copy(k, y), core_copy(k, 1 - y, n_outer + k, columns)))
+        (
+            0,
+            n_outer,
+            lambda k: (
+                inner_copy(k, y),
+                core_copy(k, y, k, columns),
+                core_copy(k, 1 - y, n_outer + k, columns),
+            ),
+        )
     )
 
     @pl.loop(1, n_outer)
@@ -269,7 +263,7 @@
         inner_copy(k, 1 - y).wait_recv()
         core_copy(k, 1 - y, n_outer + k, columns).start()
 
-    @pl.loop(1, n_outer)
+    @pl.loop(0, n_outer)
     def _(k):
         core_copy(k, y, k, columns_other).wait_recv()
 
@@ -283,7 +277,7 @@
         return send(
             score_own.at[seq],
             score_other.at[seq],
-            score_send.at[seq],
+            all_sent,
             score_recv.at[seq],
             dp,
             1 - v,
@@ -325,22 +319,25 @@
             logit_grad, picked[seq], (((1,), (0,)), ((), ())), preferred_element_type=F32
         ).reshape(n_dp, 2 * own_rows, half)
 
+    for copy in state_copies:
+        copy.start()
+
     def rs_core(k, y_of):
         return send(
             grads.at[at(fwd(k), y_of, 1 - c)],
             got_core.at[k, y_of],
-            rs_core_send.at[k, y_of],
+            all_sent,
             rs_core_recv.at[k, y_of],
             partner,
             v,
         )
 
     def rs_y(k):
-        return send(send_y.at[k], got_y.at[k], rs_y_send.at[k], rs_y_recv.at[k], other_y, v)
+        return send(send_y.at[k], got_y.at[k], all_sent, rs_y_recv.at[k], other_y, v)
 
     def rs_z(k):
         return send(
-            send_z.at[k], got_z.at[k], rs_z_send.at[k], rs_z_recv.at[k], at(fwd(k), y, c), v
+            send_z.at[k], got_z.at[k], all_sent, rs_z_recv.at[k], at(fwd(k), y, c), v
         )
 
     sent.append((0, n_outer, lambda k: (rs_core(k, 0), rs_core(k, 1), rs_y(k))))
@@ -382,7 +379,7 @@
     grad_near = jnp.where(v == 0, low, high)
     grad_far = jnp.where(v == 0, high, low)
     send_x[...] = grad_far
-    x_copy = send(send_x, grad_x, x_send, x_recv, dp, 1 - v)
+    x_copy = send(send_x, grad_x, all_sent, x_recv, dp, 1 - v)
     x_copy.start()
     sent.append((0, 1, lambda k: (x_copy,)))
     load_m.wait()
@@ -420,51 +417,38 @@
     )
     sums_own[0] = near
 
-    def sum_far(k, to, slot_of):
-        return send(
-            sums_own.at[1], sums.at[1, slot_of], sum_send.at[1, k], sum_recv.at[1, k], to, 1 - v
-        )
-
-    def sum_near(k, to, slot_of):
-        return send(
-            sums_own.at[0], sums.at[0, slot_of], sum_send.at[0, k], sum_recv.at[0, k], to, v
-        )
+    def sum_far(to):
+        return send(sums_own.at[1], sums.at[n_dp + dp], all_sent, sum_recv, to, 1 - v)
+
+    def sum_near(to):
+        return send(sums_own.at[0], sums.at[dp], all_sent, sum_recv, to, v)
 
     def to_dp(k):
         return lax.rem(dp + k, n_dp)
 
-    def from_dp(k):
-        return lax.rem(dp + n_dp - k, n_dp)
-
-    sums[0, dp] = near
+    sums[dp] = near
 
     @pl.loop(1, n_dp)
     def _(n):
         k = jnp.where(z < n_outer // 2, n_dp - n, n)
-        sum_far(k, to_dp(k), dp).start()
-        sum_near(k, to_dp(k), dp).start()
-
-    sum_far(0, dp, dp).start()
-
-    sent.append((0, n_dp, lambda k: (sum_far(k, to_dp(k), dp),)))
-    sent.append((1, n_dp, lambda k: (sum_near(k, to_dp(k), dp),)))
+        sum_far(to_dp(k)).start()
+        sum_near(to_dp(k)).start()
+
+    sum_far(dp).start()
+
+    sent.append((0, n_dp, lambda k: (sum_far(to_dp(k)),)))
+    sent.append((1, n_dp, lambda k: (sum_near(to_dp(k)),)))
     x_copy.wait_recv()
     finish_half(grad_x[...], 1 - v)
-
-    @pl.loop(0, n_dp)
-    def _(k):
-        sum_far(k, to_dp(k), from_dp(k)).wait_recv()
-
-    @pl.loop(1, n_dp)
-    def _(k):
-        sum_near(k, to_dp(k), from_dp(k)).wait_recv()
-
-    totals = jnp.sum(jnp.sum(sums[...], axis=0), axis=0)
+    finish()
+    arrivals = sums.at[pl.ds(0, 2 * n_dp - 1)]
+    send(arrivals, arrivals, all_sent, sum_recv, dp, 1 - v).wait_recv()
+
+    totals = jnp.sum(sums[...], axis=0)
     update_total = jnp.sum(jnp.where(lane == 0, totals, 0.0), axis=1, keepdims=True)
     weight_total = jnp.sum(jnp.where(lane == 1, totals, 0.0), axis=1, keepdims=True)
     trust = jnp.sqrt(weight_total) / (jnp.sqrt(update_total) + TRUST_EPSILON)
     new_head_ref[0] = head_ref[0] - LEARNING_RATE * trust * update_buf[...]
-    finish()
 
 
 def store_kernel(*refs):
@@ -485,6 +469,7 @@
     own_rows, width = head.shape[1], head.shape[2]
     n_outer = n_dp // (CORES * INNER)
     pair = 2 * own_rows
+    part = half // CORES
     block = n_dp * pair
     vmem = pl.BlockSpec(memory_space=pltpu.VMEM)
     anywhere = pl.BlockSpec(memory_space=pltpu.HBM)
@@ -502,8 +487,8 @@
         scratch_shapes=[
             pltpu.VMEM((seqs, length, half), BF16),
             pltpu.VMEM((seqs, masked, half), BF16),
-            pltpu.VMEM((2 * CORES, own_rows, half), F32),
-            pltpu.VMEM((2 * CORES * own_rows, half), F32),
+            pltpu.VMEM((2 * CORES, own_rows, part), F32),
+            pltpu.VMEM((2 * CORES * own_rows, part), F32),
             pltpu.VMEM((n_dp // CORES, CORES * pair, half), BF16),
             pltpu.VMEM((seqs, masked, block), F32),
             pltpu.VMEM((seqs, masked, block), F32),
@@ -524,30 +509,20 @@
             pltpu.VMEM(head.shape, F32),
             pltpu.VMEM((own_rows, width), F32),
             pltpu.VMEM((2, 1, 128), F32),
-            pltpu.VMEM((2, n_dp, 1, 128), F32),
+            pltpu.VMEM((2 * n_dp, 1, 128), F32),
             dma((seqs,)),
             dma((6,)),
-            dma((3,)),
+            dma,
             dma((2 * CORES,)),
             dma((n_outer,)),
             dma((n_outer,)),
-            dma((n_outer,)),
-            dma((n_outer,)),
-            dma((2 * n_outer,)),
             dma((2 * n_outer,)),
             dma((seqs,)),
-            dma((seqs,)),
             dma((n_outer, INNER)),
-            dma((n_outer, INNER)),
-            dma((n_outer,)),
-            dma((n_outer,)),
             dma((n_outer,)),
             dma((n_outer,)),
             dma,
             dma,
-            dma((2, n_dp)),
-            dma((2, n_dp)),
-            dma((2,)),
             dma((2,)),
         ],
         compiler_params=pltpu.CompilerParams(

time: 44.1 us -> 42.3 us (0.959)
  Pallas kernels: 43.3 us -> 41.5 us
    pallas_call x1, Pallas kernels: 42.6 us -> 40.8 us  [fused_step(): pl.pallas_call(functools.partial(step_kernel, n_dp), out_shape=(jax.Shape...]
where the time goes in v1:
time: 42.3 us; the launch traced here: 42.2 us
  Pallas kernels  41.5 us (98%)
  between operations  0.64 us (2%)
    pallas_call x1, Pallas kernels, fused_step(): pl.pallas_call(functools.partial(step_kernel, n_dp), out_shape=(jax.Shape...  40.8 us

profile of v1, /device:TPU:0, one launch (start us, length us, event | category | flops | bytes accessed | tf_op | source)
XLA Modules:
  0.0 42.2 jit_solution(12779651467662856735)
XLA Ops:
  0.6 40.8 %fused_step.1 = (f32[5,80]{1,0:T(8,128)S(1)}, f32[1,4,4096]{2,1,0:T(4,128)S(1)}, f32[1,4,4096]{2,1,0:T(4,128)S(1)}, f32[1,4,4096]{2,1,0:T(4,128)S(1)}) custom-call(bf16[5,512,2048]{2,1,0:T(8,128)(2,1)} %hidden_ref.1, s32[5,80]{1,0:T(8,128)} %positions_hbm.1, s32[5,80]{1,0:T(8,128)} %labels_hbm.1, f32[5,80]{1,0:T(8,128)} %lse_hbm.1, f32[1,4,4096]{2,1,0:T(4,128)} %head_hbm.1, ...), custom_call_target="tpu_custom_call" | custom-call | tf_op jit(solution)/shard_map/fused_step/pallas_call | solution.py:482
  41.5 0.7 %store_results.1 = (f32[5,80]{1,0:T(8,128)}, f32[1,4,4096]{2,1,0:T(4,128)}, f32[1,4,4096]{2,1,0:T(4,128)}, f32[1,4,4096]{2,1,0:T(4,128)}) custom-call(f32[5,80]{1,0:T(8,128)S(1)} %get-tuple-element.8.refs_0_, f32[1,4,4096]{2,1,0:T(4,128)S(1)} %get-tuple-element.9.refs_1_, f32[1,4,4096]{2,1,0:T(4,128)S(1)} %get-tuple-element.10.refs_2_, ...), custom_call_target="tpu_custom_call" | custom-call | tf_op jit(solution)/shard_map/store_results/pallas_call | solution.py:534

commit v2 on v1

--- a/solution.py
+++ b/solution.py
@@ -37,8 +37,7 @@
     tokens,
     picked,
     pieces,
-    stage,
-    rows16,
+    across,
     score_own,
     score_other,
     grads,
@@ -62,7 +61,7 @@
     load_sem,
     state_sem,
     all_sent,
-    head_recv,
+    x_head_recv,
     outer_recv,
     inner_recv,
     core_recv,
@@ -78,7 +77,6 @@
     seqs, length, half = hidden_ref.shape
     masked = positions_ref.shape[1]
     own_rows = head_ref.shape[1]
-    part = half // CORES
     dp = lax.axis_index("dp")
     v = lax.axis_index("vocab")
     c = lax.rem(dp, CORES)
@@ -88,11 +86,11 @@
     def at(z_to, y_to, c_to):
         return (z_to * INNER + y_to) * CORES + c_to
 
+    def spot(z_of, y_of, c_of):
+        return (y_of * CORES + c_of) * n_outer + z_of
+
     def fwd(k):
         return lax.rem(z + k, n_outer)
-
-    def back(k):
-        return lax.rem(z + n_outer - k, n_outer)
 
     def near_last(n):
         return jnp.where(z < n_outer // 2, n_outer - n, n)
@@ -148,7 +146,7 @@
     greet(other_y, v)
     greet(partner, v)
     greet(dp, 1 - v)
-    greet(partner, 1 - v)
+
     def pick(seq):
         load(seq).wait()
         spots = positions_ref[pl.ds(seq, 1), :]
@@ -165,21 +163,86 @@
         def _(seq):
             pick(seq)
 
+    load_head.wait()
+    pl.semaphore_wait(barrier, n_outer + 2)
+
+    def pair(z_of, y_of, c_of):
+        return pieces.at[spot(z_of, y_of, c_of)]
+
+    def piece(z_of, slab):
+        return pair(z_of, y, c).at[slab]
+
+    def half_of(h):
+        return head_ref[0, :, pl.ds(pl.multiple_of(h * half, half), half)].astype(BF16)
+
+    def x_head():
+        return send(across, piece(z, v), all_sent, x_head_recv, dp, 1 - v)
+
+    def outer_copy(z_to, slab):
+        ref = piece(z, slab)
+        return send(ref, ref, all_sent, outer_recv.at[z], at(z_to, y, c), v)
+
+    def inner_copy(z_of):
+        ref = pair(z_of, y, c)
+        return send(ref, ref, all_sent, inner_recv.at[z_of], other_y, v)
+
+    def core_copy(z_of, y_of):
+        ref = pair(z_of, y_of, c)
+        return send(ref, ref, all_sent, core_recv.at[y_of], partner, v)
+
+    def others(d, step):
+        for other in (z - d, z + d):
+
+            @pl.when((other >= 0) & (other < n_outer))
+            def _(other=other):
+                step(other)
+
+    def far_first(step):
+        @pl.loop(1, n_outer)
+        def _(n):
+            others(n_outer - n, step)
+
+    def near_first(step):
+        @pl.loop(1, n_outer)
+        def _(d):
+            others(d, step)
+
+    early, late = 2 * seqs // 5, 4 * seqs // 5
+    across[...] = half_of(1 - v)
+    pieces[spot(z, y, c), v] = half_of(v)
+    x_head().start()
+    far_first(lambda z_to: outer_copy(z_to, v).start())
     load_positions.wait()
-    load_head.wait()
-    pl.semaphore_wait(barrier, n_outer + 3)
-
-    def head_part(v_of, c_of):
-        start = pl.multiple_of(v_of * half + c_of * part, part)
-        return head_ref.at[0, :, pl.ds(start, part)]
-
-    slot = 2 * c + v
-    head_copies = [
-        send(head_part(v_to, c_to), pieces.at[slot], all_sent, head_recv.at[slot], at(z, y, c_to), v_to)
-        for v_to, c_to in ((1 - v, c), (1 - v, 1 - c), (v, 1 - c))
-    ]
-    for copy in head_copies:
-        copy.start()
+    picks(0, early)
+    whole_head = head_ref[0]
+    weight_part = jnp.sum(whole_head * whole_head, axis=(0, 1), keepdims=True)
+    send(across, piece(z, 1 - v), all_sent, x_head_recv, dp, 1 - v).wait_recv()
+    far_first(lambda z_to: outer_copy(z_to, 1 - v).start())
+    inner_copy(z).start()
+    core_copy(z, y).start()
+    picks(early, late)
+
+    def pass_on(z_from):
+        ref = pair(z_from, y, c)
+        send(ref, ref, all_sent, outer_recv.at[z_from], dp, 1 - v).wait_recv()
+        inner_copy(z_from).start()
+        core_copy(z_from, y).start()
+
+    near_first(pass_on)
+    picks(late, seqs)
+    load_labels.wait()
+    load_lse.wait()
+
+    def pass_core(z_from):
+        ref = pair(z_from, 1 - y, c)
+        send(ref, ref, all_sent, inner_recv.at[z_from], dp, 1 - v).wait_recv()
+        core_copy(z_from, 1 - y).start()
+
+    pass_core(z)
+    near_first(pass_core)
+    for y_of in (y, 1 - y):
+        ref = pieces.at[pl.ds(spot(0, y_of, 1 - c), n_outer)]
+        send(ref, ref, all_sent, core_recv.at[y_of], dp, 1 - v).wait_recv()
 
     def state_cols(ref):
         return ref.at[0, :, pl.ds(pl.multiple_of((1 - v) * half, half), half)]
@@ -188,88 +251,9 @@
         send(state_cols(m_ref), state_far.at[0], all_sent, far_recv.at[0], dp, 1 - v),
         send(state_cols(v_ref), state_far.at[1], all_sent, far_recv.at[1], dp, 1 - v),
     ]
-    sent.append((0, 1, lambda k: head_copies + state_copies))
-    pieces[slot] = head_ref[0, :, pl.ds(pl.multiple_of(v * half + c * part, part), part)]
-    whole_head = head_ref[0]
-    weight_part = jnp.sum(whole_head * whole_head, axis=(0, 1), keepdims=True)
-
-    picks(0, 1)
-    for slot_from in (
-        2 * (1 - c) + v,
-        2 * c + 1 - v,
-        2 * (1 - c) + 1 - v,
-    ):
-        send(
-            head_part(0, 0), pieces.at[slot_from], all_sent, head_recv.at[slot_from], dp, 1 - v
-        ).wait_recv()
-    for k in range(2 * CORES):
-        stage[k * own_rows : (k + 1) * own_rows, :] = pieces[k]
-    columns = pl.ds(pl.multiple_of(c * part, part), part)
-    rows16[z * INNER + y, :, columns] = stage[...].astype(BF16)
-    columns_other = pl.ds(pl.multiple_of((1 - c) * part, part), part)
-
-    def rows_of(z_of, y_of, cols):
-        return rows16.at[z_of * INNER + y_of, :, cols]
-
-    def outer_copy(k, z_of):
-        ref = rows_of(z_of, y, columns)
-        return send(ref, ref, all_sent, outer_recv.at[k], at(fwd(k), y, c), v)
-
-    def inner_copy(k, y_of):
-        ref = rows_of(back(k), y_of, columns)
-        return send(ref, ref, all_sent, inner_recv.at[k], other_y, v)
-
-    def core_copy(k, y_of, index, cols):
-        ref = rows_of(back(k), y_of, cols)
-        return send(ref, ref, all_sent, core_recv.at[index], partner, v)
-
-    inner_copy(0, y).start()
-    core_copy(0, y, 0, columns).start()
-    sent.append((1, n_outer, lambda k: (outer_copy(k, z),)))
-    sent.append(
-        (
-            0,
-            n_outer,
-            lambda k: (
-                inner_copy(k, y),
-                core_copy(k, y, k, columns),
-                core_copy(k, 1 - y, n_outer + k, columns),
-            ),
-        )
-    )
-
-    @pl.loop(1, n_outer)
-    def _(n):
-        outer_copy(near_last(n), z).start()
-
-    picks(1, seqs)
-
-    @pl.loop(1, n_outer)
-    def _(n):
-        k = near_last(n)
-        outer_copy(k, back(k)).wait_recv()
-        inner_copy(k, y).start()
-        core_copy(k, y, k, columns).start()
-
-    load_labels.wait()
-    load_lse.wait()
-
-    inner_copy(0, 1 - y).wait_recv()
-    core_copy(0, 1 - y, n_outer, columns).start()
-
-    @pl.loop(1, n_outer)
-    def _(n):
-        k = near_last(n)
-        inner_copy(k, 1 - y).wait_recv()
-        core_copy(k, 1 - y, n_outer + k, columns).start()
-
-    @pl.loop(0, n_outer)
-    def _(k):
-        core_copy(k, y, k, columns_other).wait_recv()
-
-    @pl.loop(0, n_outer)
-    def _(k):
-        core_copy(k, 1 - y, n_outer + k, columns_other).wait_recv()
+    sent.append((0, 1, lambda k: state_copies + [x_head()]))
+    sent.append((1, n_outer, lambda k: (outer_copy(z, 0), outer_copy(z, 1))))
+    sent.append((0, n_outer, lambda k: (inner_copy(k), core_copy(k, 0), core_copy(k, 1))))
 
     block = n_dp * 2 * own_rows
 
@@ -287,7 +271,7 @@
     def _(seq):
         score_own[seq] = lax.dot_general(
             picked[seq],
-            rows16[...].reshape(block, half),
+            pieces[...].reshape(block, half),
             (((1,), (1,)), ((), ())),
             preferred_element_type=F32,
         )
@@ -297,9 +281,14 @@
     grads[...] = jnp.zeros_like(grads)
     row = lax.broadcasted_iota(jnp.int32, (block, masked), 0)
     shift = own_rows.bit_length() - 1
+    slot = lax.shift_right_logical(row, shift + 1)
+    outer_bits = n_outer.bit_length() - 1
+    slot_z = slot & (n_outer - 1)
+    slot_c = lax.shift_right_logical(slot, outer_bits) & (CORES - 1)
+    slot_y = lax.shift_right_logical(slot, outer_bits + CORES.bit_length() - 1)
     row_id = (
         (lax.shift_right_logical(row, shift) & 1) * (n_dp * own_rows)
-        + lax.shift_right_logical(row, shift + 1) * own_rows
+        + at(slot_z, slot_y, slot_c) * own_rows
         + (row & (own_rows - 1))
     )
 
@@ -324,7 +313,7 @@
 
     def rs_core(k, y_of):
         return send(
-            grads.at[at(fwd(k), y_of, 1 - c)],
+            grads.at[spot(fwd(k), y_of, 1 - c)],
             got_core.at[k, y_of],
             all_sent,
             rs_core_recv.at[k, y_of],
@@ -358,7 +347,7 @@
     def _(n):
         k = later(n)
         rs_core(k, 1 - y).wait_recv()
-        send_y[k] = grads[at(fwd(k), 1 - y, c)] + got_core[k, 1 - y]
+        send_y[k] = grads[spot(fwd(k), 1 - y, c)] + got_core[k, 1 - y]
         rs_y(k).start()
 
     @pl.loop(1, n_outer)
@@ -366,12 +355,12 @@
         k = near_last(n)
         rs_core(k, y).wait_recv()
         rs_y(k).wait_recv()
-        send_z[k] = grads[at(fwd(k), y, c)] + got_core[k, y] + got_y[k]
+        send_z[k] = grads[spot(fwd(k), y, c)] + got_core[k, y] + got_y[k]
         rs_z(k).start()
 
     rs_core(0, y).wait_recv()
     rs_y(0).wait_recv()
-    rows8 = grads[at(z, y, c)] + got_core[0, y] + got_y[0]
+    rows8 = grads[spot(z, y, c)] + got_core[0, y] + got_y[0]
     for k in range(1, n_outer):
         rs_z(k).wait_recv()
         rows8 = rows8 + got_z[k]
@@ -469,7 +458,6 @@
     own_rows, width = head.shape[1], head.shape[2]
     n_outer = n_dp // (CORES * INNER)
     pair = 2 * own_rows
-    part = half // CORES
     block = n_dp * pair
     vmem = pl.BlockSpec(memory_space=pltpu.VMEM)
     anywhere = pl.BlockSpec(memory_space=pltpu.HBM)
@@ -487,9 +475,8 @@
         scratch_shapes=[
             pltpu.VMEM((seqs, length, half), BF16),
             pltpu.VMEM((seqs, masked, half), BF16),
-            pltpu.VMEM((2 * CORES, own_rows, part), F32),
-            pltpu.VMEM((2 * CORES * own_rows, part), F32),
-            pltpu.VMEM((n_dp // CORES, CORES * pair, half), BF16),
+            pltpu.VMEM((n_dp, 2, own_rows, half), BF16),
+            pltpu.VMEM((own_rows, half), BF16),
             pltpu.VMEM((seqs, masked, block), F32),
             pltpu.VMEM((seqs, masked, block), F32),
             pltpu.VMEM((n_dp, pair, half), F32),
@@ -513,10 +500,10 @@
             dma((seqs,)),
             dma((6,)),
             dma,
-            dma((2 * CORES,)),
+            dma,
             dma((n_outer,)),
             dma((n_outer,)),
-            dma((2 * n_outer,)),
+            dma((INNER,)),
             dma((seqs,)),
             dma((n_outer, INNER)),
             dma((n_outer,)),
@@ -604,6 +591,8 @@
     n_dp, n_vocab = mesh.shape["dp"], mesh.shape["vocab"]
     own_rows = args[4].shape[1] // n_dp
     power_of_two = own_rows & (own_rows - 1) == 0
+    n_outer = n_dp // (CORES * INNER)
+    power_of_two = power_of_two and n_outer & (n_outer - 1) == 0
     return n_vocab == 2 and n_dp % (CORES * INNER) == 0 and power_of_two
 
 

time: 42.3 us -> 41.3 us (0.976)
  Pallas kernels: 41.5 us -> 40.5 us
    pallas_call x1, Pallas kernels: 40.8 us -> 39.8 us  [fused_step(): pl.pallas_call(functools.partial(step_kernel, n_dp), out_shape=(jax.Shape...]
where the time goes in v2:
time: 41.3 us; the launch traced here: 41.1 us
  Pallas kernels  40.5 us (98%)
  between operations  0.64 us (2%)
    pallas_call x1, Pallas kernels, fused_step(): pl.pallas_call(functools.partial(step_kernel, n_dp), out_shape=(jax.Shape...  39.8 us

profile of v2, /device:TPU:0, one launch (start us, length us, event | category | flops | bytes accessed | tf_op | source)
XLA Modules:
  0.0 41.1 jit_solution(12984084624938997741)
XLA Ops:
  0.6 39.8 %fused_step.1 = (f32[5,80]{1,0:T(8,128)S(1)}, f32[1,4,4096]{2,1,0:T(4,128)S(1)}, f32[1,4,4096]{2,1,0:T(4,128)S(1)}, f32[1,4,4096]{2,1,0:T(4,128)S(1)}) custom-call(bf16[5,512,2048]{2,1,0:T(8,128)(2,1)} %hidden_ref.1, s32[5,80]{1,0:T(8,128)} %positions_hbm.1, s32[5,80]{1,0:T(8,128)} %labels_hbm.1, f32[5,80]{1,0:T(8,128)} %lse_hbm.1, f32[1,4,4096]{2,1,0:T(4,128)} %head_hbm.1, ...), custom_call_target="tpu_custom_call" | custom-call | tf_op jit(solution)/shard_map/fused_step/pallas_call | solution.py:470
  40.4 0.7 %store_results.1 = (f32[5,80]{1,0:T(8,128)}, f32[1,4,4096]{2,1,0:T(4,128)}, f32[1,4,4096]{2,1,0:T(4,128)}, f32[1,4,4096]{2,1,0:T(4,128)}) custom-call(f32[5,80]{1,0:T(8,128)S(1)} %get-tuple-element.8.refs_0_, f32[1,4,4096]{2,1,0:T(4,128)S(1)} %get-tuple-element.9.refs_1_, f32[1,4,4096]{2,1,0:T(4,128)S(1)} %get-tuple-element.10.refs_2_, ...), custom_call_target="tpu_custom_call" | custom-call | tf_op jit(solution)/shard_map/store_results/pallas_call | solution.py:521

commit v3 on v2

--- a/solution.py
+++ b/solution.py
@@ -40,6 +40,8 @@
     across,
     score_own,
     score_other,
+    tail_own,
+    tail_other,
     grads,
     got_core,
     send_y,
@@ -66,6 +68,7 @@
     inner_recv,
     core_recv,
     score_recv,
+    tail_recv,
     rs_core_recv,
     rs_y_recv,
     rs_z_recv,
@@ -238,11 +241,68 @@
         send(ref, ref, all_sent, inner_recv.at[z_from], dp, 1 - v).wait_recv()
         core_copy(z_from, 1 - y).start()
 
-    pass_core(z)
-    near_first(pass_core)
-    for y_of in (y, 1 - y):
+    def core_wait(y_of):
         ref = pieces.at[pl.ds(spot(0, y_of, 1 - c), n_outer)]
         send(ref, ref, all_sent, core_recv.at[y_of], dp, 1 - v).wait_recv()
+
+    block = n_dp * 2 * own_rows
+    side = block // INNER
+    pairs, odd = seqs // 2, seqs % 2
+    cut = masked // 2
+
+    def score_part(y_of, seq, count):
+        near = pieces[pl.ds(y_of * (n_dp // INNER), n_dp // INNER)].reshape(side, half)
+        return lax.dot_general(
+            picked[pl.ds(seq, count)].reshape(count * masked, half),
+            near,
+            (((1,), (1,)), ((), ())),
+            preferred_element_type=F32,
+        )
+
+    def score_copy(y_of, m):
+        return send(
+            score_own.at[y_of, m],
+            score_other.at[y_of, m],
+            all_sent,
+            score_recv.at[y_of, m],
+            dp,
+            1 - v,
+        )
+
+    def tail_copy(y_of):
+        return send(tail_own.at[y_of], tail_other.at[y_of], all_sent, tail_recv.at[y_of], dp, 1 - v)
+
+    def send_pair(y_of, m):
+        both = score_part(y_of, 2 * m, 2)
+        score_own[y_of, m] = jnp.concatenate([both[:masked], both[masked:]], axis=1)
+        score_copy(y_of, m).start()
+
+    def send_tail(y_of):
+        last = score_part(y_of, seqs - 1, 1)
+        tail_own[y_of] = jnp.concatenate([last[:cut], last[cut:]], axis=1)
+        tail_copy(y_of).start()
+
+    tasks = [functools.partial(send_pair, y, m) for m in range(pairs)]
+    if odd:
+        tasks.append(functools.partial(send_tail, y))
+    pass_core(z)
+    core_wait(y)
+    for d in range(1, n_outer):
+        if tasks:
+            tasks.pop(0)()
+        others(d, pass_core)
+    for task in tasks:
+        task()
+    core_wait(1 - y)
+
+    @pl.loop(0, pairs)
+    def _(m):
+        send_pair(1 - y, m)
+
+    if odd:
+        send_tail(1 - y)
+        sent.append((0, INNER, lambda k: (tail_copy(k),)))
+    sent.append((0, pairs, lambda m: (score_copy(0, m), score_copy(1, m))))
 
     def state_cols(ref):
         return ref.at[0, :, pl.ds(pl.multiple_of((1 - v) * half, half), half)]
@@ -255,29 +315,6 @@
     sent.append((1, n_outer, lambda k: (outer_copy(z, 0), outer_copy(z, 1))))
     sent.append((0, n_outer, lambda k: (inner_copy(k), core_copy(k, 0), core_copy(k, 1))))
 
-    block = n_dp * 2 * own_rows
-
-    def score_copy(seq):
-        return send(
-            score_own.at[seq],
-            score_other.at[seq],
-            all_sent,
-            score_recv.at[seq],
-            dp,
-            1 - v,
-        )
-
-    @pl.loop(0, seqs)
-    def _(seq):
-        score_own[seq] = lax.dot_general(
-            picked[seq],
-            pieces[...].reshape(block, half),
-            (((1,), (1,)), ((), ())),
-            preferred_element_type=F32,
-        )
-        score_copy(seq).start()
-
-    sent.append((0, seqs, lambda seq: (score_copy(seq),)))
     grads[...] = jnp.zeros_like(grads)
     row = lax.broadcasted_iota(jnp.int32, (block, masked), 0)
     shift = own_rows.bit_length() - 1
@@ -292,10 +329,7 @@
         + (row & (own_rows - 1))
     )
 
-    @pl.loop(0, seqs)
-    def _(seq):
-        score_copy(seq).wait_recv()
-        scores = jnp.transpose(score_own[seq] + score_other[seq])
+    def finish_seq(seq, scores):
         rest = lse_ref[pl.ds(seq, 1), :]
         top = jnp.maximum(jnp.max(scores, axis=0, keepdims=True), rest)
         total = jnp.exp(rest - top) + jnp.sum(jnp.exp(scores - top), axis=0, keepdims=True)
@@ -307,6 +341,24 @@
         grads[...] += lax.dot_general(
             logit_grad, picked[seq], (((1,), (0,)), ((), ())), preferred_element_type=F32
         ).reshape(n_dp, 2 * own_rows, half)
+
+    @pl.loop(0, pairs)
+    def _(m):
+        turned = []
+        for y_of in range(INNER):
+            score_copy(y_of, m).wait_recv()
+            turned.append(jnp.transpose(score_own[y_of, m] + score_other[y_of, m]))
+        for n in range(2):
+            rows = slice(n * side, (n + 1) * side)
+            finish_seq(2 * m + n, jnp.concatenate([t[rows] for t in turned], axis=0))
+
+    if odd:
+        turned = []
+        for y_of in range(INNER):
+            tail_copy(y_of).wait_recv()
+            turned.append(jnp.transpose(tail_own[y_of] + tail_other[y_of]))
+        sides = [jnp.concatenate([t[n * side : (n + 1) * side] for t in turned], axis=0) for n in range(2)]
+        finish_seq(seqs - 1, jnp.concatenate(sides, axis=1))
 
     for copy in state_copies:
         copy.start()
@@ -477,8 +529,10 @@
             pltpu.VMEM((seqs, masked, half), BF16),
             pltpu.VMEM((n_dp, 2, own_rows, half), BF16),
             pltpu.VMEM((own_rows, half), BF16),
-            pltpu.VMEM((seqs, masked, block), F32),
-            pltpu.VMEM((seqs, masked, block), F32),
+            pltpu.VMEM((INNER, max(seqs // 2, 1), masked, block), F32),
+            pltpu.VMEM((INNER, max(seqs // 2, 1), masked, block), F32),
+            pltpu.VMEM((INNER, masked // 2, block), F32),
+            pltpu.VMEM((INNER, masked // 2, block), F32),
             pltpu.VMEM((n_dp, pair, half), F32),
             pltpu.VMEM((n_outer, INNER, pair, half), F32),
             pltpu.VMEM((n_outer, pair, half), F32),
@@ -504,7 +558,8 @@
             dma((n_outer,)),
             dma((n_outer,)),
             dma((INNER,)),
-            dma((seqs,)),
+            dma((INNER, max(seqs // 2, 1))),
+            dma((INNER,)),
             dma((n_outer, INNER)),
             dma((n_outer,)),
             dma((n_outer,)),
@@ -593,6 +648,8 @@
     power_of_two = own_rows & (own_rows - 1) == 0
     n_outer = n_dp // (CORES * INNER)
     power_of_two = power_of_two and n_outer & (n_outer - 1) == 0
+    masked = args[1].shape[1]
+    power_of_two = power_of_two and masked % 16 == 0
     return n_vocab == 2 and n_dp % (CORES * INNER) == 0 and power_of_two
 
 

time: 41.3 us -> 39.9 us (0.966)
  Pallas kernels: 40.5 us -> 39.2 us
    pallas_call x1, Pallas kernels: 39.8 us -> 38.4 us  [fused_step(): pl.pallas_call(functools.partial(step_kernel, n_dp), out_shape=(jax.Shape...]
where the time goes in v3:
time: 39.9 us; the launch traced here: 39.8 us
  Pallas kernels  39.2 us (98%)
  between operations  0.64 us (2%)
    pallas_call x1, Pallas kernels, fused_step(): pl.pallas_call(functools.partial(step_kernel, n_dp), out_shape=(jax.Shape...  38.4 us

profile of v3, /device:TPU:0, one launch (start us, length us, event | category | flops | bytes accessed | tf_op | source)
XLA Modules:
  0.0 39.8 jit_solution(9606408467958485480)
XLA Ops:
  0.6 38.4 %fused_step.1 = (f32[5,80]{1,0:T(8,128)S(1)}, f32[1,4,4096]{2,1,0:T(4,128)S(1)}, f32[1,4,4096]{2,1,0:T(4,128)S(1)}, f32[1,4,4096]{2,1,0:T(4,128)S(1)}) custom-call(bf16[5,512,2048]{2,1,0:T(8,128)(2,1)} %hidden_ref.1, s32[5,80]{1,0:T(8,128)} %positions_hbm.1, s32[5,80]{1,0:T(8,128)} %labels_hbm.1, f32[5,80]{1,0:T(8,128)} %lse_hbm.1, f32[1,4,4096]{2,1,0:T(4,128)} %head_hbm.1, ...), custom_call_target="tpu_custom_call" | custom-call | tf_op jit(solution)/shard_map/fused_step/pallas_call | solution.py:522
  39.1 0.7 %store_results.1 = (f32[5,80]{1,0:T(8,128)}, f32[1,4,4096]{2,1,0:T(4,128)}, f32[1,4,4096]{2,1,0:T(4,128)}, f32[1,4,4096]{2,1,0:T(4,128)}) custom-call(f32[5,80]{1,0:T(8,128)S(1)} %get-tuple-element.8.refs_0_, f32[1,4,4096]{2,1,0:T(4,128)S(1)} %get-tuple-element.9.refs_1_, f32[1,4,4096]{2,1,0:T(4,128)S(1)} %get-tuple-element.10.refs_2_, ...), custom_call_target="tpu_custom_call" | custom-call | tf_op jit(solution)/shard_map/store_results/pallas_call | solution.py:576

commit v4 on v3

--- a/solution.py
+++ b/solution.py
@@ -95,9 +95,6 @@
     def fwd(k):
         return lax.rem(z + k, n_outer)
 
-    def near_last(n):
-        return jnp.where(z < n_outer // 2, n_outer - n, n)
-
     def send(src, dst, ssem, rsem, dp_to, v_to):
         return pltpu.make_async_remote_copy(
             src_ref=src,
@@ -210,7 +207,7 @@
         def _(d):
             others(d, step)
 
-    early, late = 2 * seqs // 5, 4 * seqs // 5
+    early, late = 3 * seqs // 5, 4 * seqs // 5
     across[...] = half_of(1 - v)
     pieces[spot(z, y, c), v] = half_of(v)
     x_head().start()
@@ -363,59 +360,74 @@
     for copy in state_copies:
         copy.start()
 
-    def rs_core(k, y_of):
+    part = half // 2
+
+    def turn(n):
+        down = n_outer - 1 - n
+        low_side = jnp.where(down > z, down, down - 1)
+        high_side = jnp.where(n < z, n, n + 1)
+        return jnp.where(n == n_outer - 1, z, jnp.where(z < n_outer // 2, low_side, high_side))
+
+    def rs_core(d, y_of):
         return send(
-            grads.at[spot(fwd(k), y_of, 1 - c)],
-            got_core.at[k, y_of],
+            grads.at[spot(d, y_of, 1 - c)],
+            got_core.at[d, y_of],
             all_sent,
-            rs_core_recv.at[k, y_of],
+            rs_core_recv.at[d, y_of],
             partner,
             v,
         )
 
-    def rs_y(k):
-        return send(send_y.at[k], got_y.at[k], all_sent, rs_y_recv.at[k], other_y, v)
-
-    def rs_z(k):
+    def rs_y(d, h):
+        return send(send_y.at[d, h], got_y.at[d, h], all_sent, rs_y_recv.at[d, h], other_y, v)
+
+    def rs_z(d, h):
         return send(
-            send_z.at[k], got_z.at[k], all_sent, rs_z_recv.at[k], at(fwd(k), y, c), v
+            send_z.at[d, h], got_z.at[z, h], all_sent, rs_z_recv.at[z, h], at(d, y, c), v
         )
 
-    sent.append((0, n_outer, lambda k: (rs_core(k, 0), rs_core(k, 1), rs_y(k))))
-    sent.append((1, n_outer, lambda k: (rs_z(k),)))
-
-    def later(n):
-        return lax.rem(near_last(n + 1), n_outer) * jnp.where(n == n_outer - 1, 0, 1)
+    def chip_sum(d, y_of, h):
+        cols = slice(h * part, (h + 1) * part)
+        return grads[spot(d, y_of, c), :, cols] + got_core[d, y_of, :, cols]
+
+    sent.append((0, n_outer, lambda k: (rs_core(k, 0), rs_core(k, 1), rs_y(k, 0), rs_y(k, 1))))
+    sent.append((1, n_outer, lambda k: (rs_z(z, 0), rs_z(z, 1))))
+
+    for y_of in (1 - y, y):
+
+        @pl.loop(0, n_outer)
+        def _(n, y_of=y_of):
+            rs_core(turn(n), y_of).start()
 
     @pl.loop(0, n_outer)
     def _(n):
-        rs_core(later(n), 1 - y).start()
-
-    @pl.loop(0, n_outer)
+        d = turn(n)
+        rs_core(d, 1 - y).wait_recv()
+        for h in range(2):
+            send_y[d, h] = chip_sum(d, 1 - y, h)
+            rs_y(d, h).start()
+
+    @pl.loop(0, n_outer - 1)
     def _(n):
-        rs_core(later(n), y).start()
-
-    @pl.loop(0, n_outer)
-    def _(n):
-        k = later(n)
-        rs_core(k, 1 - y).wait_recv()
-        send_y[k] = grads[spot(fwd(k), 1 - y, c)] + got_core[k, 1 - y]
-        rs_y(k).start()
-
-    @pl.loop(1, n_outer)
-    def _(n):
-        k = near_last(n)
-        rs_core(k, y).wait_recv()
-        rs_y(k).wait_recv()
-        send_z[k] = grads[spot(fwd(k), y, c)] + got_core[k, y] + got_y[k]
-        rs_z(k).start()
-
-    rs_core(0, y).wait_recv()
-    rs_y(0).wait_recv()
-    rows8 = grads[spot(z, y, c)] + got_core[0, y] + got_y[0]
-    for k in range(1, n_outer):
-        rs_z(k).wait_recv()
-        rows8 = rows8 + got_z[k]
+        d = turn(n)
+        rs_core(d, y).wait_recv()
+        for h in range(2):
+            rs_y(d, h).wait_recv()
+            send_z[d, h] = chip_sum(d, y, h) + got_y[d, h]
+            rs_z(d, h).start()
+
+    rs_core(z, y).wait_recv()
+    row_halves = []
+    for h in range(2):
+        rs_y(z, h).wait_recv()
+        row_half = chip_sum(z, y, h) + got_y[z, h]
+        for k in range(1, n_outer):
+            z_from = fwd(k)
+            got = got_z.at[z_from, h]
+            send(got, got, all_sent, rs_z_recv.at[z_from, h], dp, 1 - v).wait_recv()
+            row_half = row_half + got_z[z_from, h]
+        row_halves.append(row_half)
+    rows8 = jnp.concatenate(row_halves, axis=1)
     low, high = rows8[:own_rows], rows8[own_rows:]
     grad_near = jnp.where(v == 0, low, high)
     grad_far = jnp.where(v == 0, high, low)
@@ -451,31 +463,33 @@
     lane = lax.broadcasted_iota(jnp.int32, (1, 128), 1)
     _, _, update_far = lamb(grad_far, state_far[0], state_far[1])
     sums_own[1] = jnp.where(lane == 0, square_sum(update_far), 0.0)
+    def sum_far(to):
+        return send(sums_own.at[1], sums.at[n_dp + dp], all_sent, sum_recv, to, 1 - v)
+
+    def sum_near(to):
+        return send(sums_own.at[0], sums.at[dp], all_sent, sum_recv, to, v)
+
+    def near_dp(n):
+        return jnp.where(z < n_outer // 2, n_dp - n, n)
+
+    def to_dp(k):
+        return lax.rem(dp + k, n_dp)
+
+    @pl.loop(0, n_dp)
+    def _(n):
+        sum_far(to_dp(near_dp(n))).start()
+
     near = jnp.where(
         lane == 0,
         square_sum(finish_half(grad_near, v)),
         jnp.where(lane == 1, weight_part, 0.0),
     )
     sums_own[0] = near
-
-    def sum_far(to):
-        return send(sums_own.at[1], sums.at[n_dp + dp], all_sent, sum_recv, to, 1 - v)
-
-    def sum_near(to):
-        return send(sums_own.at[0], sums.at[dp], all_sent, sum_recv, to, v)
-
-    def to_dp(k):
-        return lax.rem(dp + k, n_dp)
-
     sums[dp] = near
 
     @pl.loop(1, n_dp)
     def _(n):
-        k = jnp.where(z < n_outer // 2, n_dp - n, n)
-        sum_far(to_dp(k)).start()
-        sum_near(to_dp(k)).start()
-
-    sum_far(dp).start()
+        sum_near(to_dp(near_dp(n))).start()
 
     sent.append((0, n_dp, lambda k: (sum_far(to_dp(k)),)))
     sent.append((1, n_dp, lambda k: (sum_near(to_dp(k)),)))
@@ -535,10 +549,10 @@
             pltpu.VMEM((INNER, masked // 2, block), F32),
             pltpu.VMEM((n_dp, pair, half), F32),
             pltpu.VMEM((n_outer, INNER, pair, half), F32),
-            pltpu.VMEM((n_outer, pair, half), F32),
-            pltpu.VMEM((n_outer, pair, half), F32),
-            pltpu.VMEM((n_outer, pair, half), F32),
-            pltpu.VMEM((n_outer, pair, half), F32),
+            pltpu.VMEM((n_outer, 2, pair, half // 2), F32),
+            pltpu.VMEM((n_outer, 2, pair, half // 2), F32),
+            pltpu.VMEM((n_outer, 2, pair, half // 2), F32),
+            pltpu.VMEM((n_outer, 2, pair, half // 2), F32),
             pltpu.VMEM((own_rows, half), F32),
             pltpu.VMEM((own_rows, half), F32),
             pltpu.VMEM((2, own_rows, half), F32),
@@ -561,8 +575,8 @@
             dma((INNER, max(seqs // 2, 1))),
             dma((INNER,)),
             dma((n_outer, INNER)),
-            dma((n_outer,)),
-            dma((n_outer,)),
+            dma((n_outer, 2)),
+            dma((n_outer, 2)),
             dma,
             dma,
             dma((2,)),

time: 39.9 us -> 38.9 us (0.975)
  Pallas kernels: 39.2 us -> 38.1 us
    pallas_call x1, Pallas kernels: 38.4 us -> 37.4 us  [fused_step(): pl.pallas_call(functools.partial(step_kernel, n_dp), out_shape=(jax.Shape...]
where the time goes in v4:
time: 38.9 us; the launch traced here: 38.7 us
  Pallas kernels  38.1 us (98%)
  between operations  0.64 us (2%)
    pallas_call x1, Pallas kernels, fused_step(): pl.pallas_call(functools.partial(step_kernel, n_dp), out_shape=(jax.Shape...  37.4 us

profile of v4, /device:TPU:0, one launch (start us, length us, event | category | flops | bytes accessed | tf_op | source)
XLA Modules:
  0.0 38.7 jit_solution(4106964118330671416)
XLA Ops:
  0.6 37.4 %fused_step.1 = (f32[5,80]{1,0:T(8,128)S(1)}, f32[1,4,4096]{2,1,0:T(4,128)S(1)}, f32[1,4,4096]{2,1,0:T(4,128)S(1)}, f32[1,4,4096]{2,1,0:T(4,128)S(1)}) custom-call(bf16[5,512,2048]{2,1,0:T(8,128)(2,1)} %hidden_ref.1, s32[5,80]{1,0:T(8,128)} %positions_hbm.1, s32[5,80]{1,0:T(8,128)} %labels_hbm.1, f32[5,80]{1,0:T(8,128)} %lse_hbm.1, f32[1,4,4096]{2,1,0:T(4,128)} %head_hbm.1, ...), custom_call_target="tpu_custom_call" | custom-call | tf_op jit(solution)/shard_map/fused_step/pallas_call | solution.py:536
  38.0 0.7 %store_results.1 = (f32[5,80]{1,0:T(8,128)}, f32[1,4,4096]{2,1,0:T(4,128)}, f32[1,4,4096]{2,1,0:T(4,128)}, f32[1,4,4096]{2,1,0:T(4,128)}) custom-call(f32[5,80]{1,0:T(8,128)S(1)} %get-tuple-element.8.refs_0_, f32[1,4,4096]{2,1,0:T(4,128)S(1)} %get-tuple-element.9.refs_1_, f32[1,4,4096]{2,1,0:T(4,128)S(1)} %get-tuple-element.10.refs_2_, ...), custom_call_target="tpu_custom_call" | custom-call | tf_op jit(solution)/shard_map/store_results/pallas_call | solution.py:590

commit v5 on v4

--- a/solution.py
+++ b/solution.py
@@ -44,6 +44,11 @@
     tail_other,
     grads,
     got_core,
+    last_got_core,
+    last_send_z,
+    last_got_z,
+    last_send_y,
+    last_got_y,
     send_y,
     got_y,
     send_z,
@@ -70,6 +75,9 @@
     score_recv,
     tail_recv,
     rs_core_recv,
+    last_core_recv,
+    last_z_recv,
+    last_y_recv,
     rs_y_recv,
     rs_z_recv,
     x_recv,
@@ -180,10 +188,10 @@
 
     def outer_copy(z_to, slab):
         ref = piece(z, slab)
-        return send(ref, ref, all_sent, outer_recv.at[z], at(z_to, y, c), v)
-
-    def inner_copy(z_of):
-        ref = pair(z_of, y, c)
+        return send(ref, ref, all_sent, outer_recv.at[z, slab], at(z_to, y, c), v)
+
+    def inner_copy(z_of, slab):
+        ref = piece(z_of, slab)
         return send(ref, ref, all_sent, inner_recv.at[z_of], other_y, v)
 
     def core_copy(z_of, y_of):
@@ -212,22 +220,27 @@
     pieces[spot(z, y, c), v] = half_of(v)
     x_head().start()
     far_first(lambda z_to: outer_copy(z_to, v).start())
+    inner_copy(z, v).start()
     load_positions.wait()
     picks(0, early)
     whole_head = head_ref[0]
     weight_part = jnp.sum(whole_head * whole_head, axis=(0, 1), keepdims=True)
     send(across, piece(z, 1 - v), all_sent, x_head_recv, dp, 1 - v).wait_recv()
     far_first(lambda z_to: outer_copy(z_to, 1 - v).start())
-    inner_copy(z).start()
+    inner_copy(z, 1 - v).start()
     core_copy(z, y).start()
     picks(early, late)
 
+    def pass_piece(z_from, slab):
+        ref = piece(z_from, slab)
+        send(ref, ref, all_sent, outer_recv.at[z_from, slab], dp, 1 - v).wait_recv()
+        inner_copy(z_from, slab).start()
+
     def pass_on(z_from):
-        ref = pair(z_from, y, c)
-        send(ref, ref, all_sent, outer_recv.at[z_from], dp, 1 - v).wait_recv()
-        inner_copy(z_from).start()
+        pass_piece(z_from, 1 - v)
         core_copy(z_from, y).start()
 
+    near_first(lambda z_from: pass_piece(z_from, v))
     near_first(pass_on)
     picks(late, seqs)
     load_labels.wait()
@@ -310,7 +323,7 @@
     ]
     sent.append((0, 1, lambda k: state_copies + [x_head()]))
     sent.append((1, n_outer, lambda k: (outer_copy(z, 0), outer_copy(z, 1))))
-    sent.append((0, n_outer, lambda k: (inner_copy(k), core_copy(k, 0), core_copy(k, 1))))
+    sent.append((0, n_outer, lambda k: (inner_copy(k, 0), inner_copy(k, 1), core_copy(k, 0), core_copy(k, 1))))
 
     grads[...] = jnp.zeros_like(grads)
     row = lax.broadcasted_iota(jnp.int32, (block, masked), 0)
@@ -360,7 +373,9 @@
     for copy in state_copies:
         copy.start()
 
-    part = half // 2
+    quarter = half // 4
+    main = half - quarter
+    part = main // 2
 
     def turn(n):
         down = n_outer - 1 - n
@@ -370,7 +385,7 @@
 
     def rs_core(d, y_of):
         return send(
-            grads.at[spot(d, y_of, 1 - c)],
+            grads.at[spot(d, y_of, 1 - c), :, pl.ds(0, main)],
             got_core.at[d, y_of],
             all_sent,
             rs_core_recv.at[d, y_of],
@@ -390,22 +405,62 @@
         cols = slice(h * part, (h + 1) * part)
         return grads[spot(d, y_of, c), :, cols] + got_core[d, y_of, :, cols]
 
+    def last_core(y_of):
+        return send(
+            grads.at[pl.ds(spot(0, y_of, 1 - c), n_outer), :, pl.ds(main, quarter)],
+            last_got_core.at[y_of],
+            all_sent,
+            last_core_recv.at[y_of],
+            partner,
+            v,
+        )
+
+    def last_z(d):
+        return send(
+            last_send_z.at[d], last_got_z.at[z], all_sent, last_z_recv.at[z], at(d, y, c), v
+        )
+
+    def last_sum(d, y_of):
+        return grads[spot(d, y_of, c), :, pl.ds(main, quarter)] + last_got_core[y_of, d]
+
+    last_y = send(last_send_y, last_got_y, all_sent, last_y_recv, other_y, v)
     sent.append((0, n_outer, lambda k: (rs_core(k, 0), rs_core(k, 1), rs_y(k, 0), rs_y(k, 1))))
-    sent.append((1, n_outer, lambda k: (rs_z(z, 0), rs_z(z, 1))))
-
-    for y_of in (1 - y, y):
-
-        @pl.loop(0, n_outer)
-        def _(n, y_of=y_of):
-            rs_core(turn(n), y_of).start()
+    sent.append((1, n_outer, lambda k: (rs_z(z, 0), rs_z(z, 1), last_z(z))))
+    sent.append((0, 1, lambda k: (last_core(0), last_core(1), last_y)))
+
+    rs_core(turn(0), 1 - y).start()
+    for y_of in range(INNER):
+        last_core(y_of).start()
+
+    @pl.loop(1, n_outer)
+    def _(n):
+        rs_core(turn(n), 1 - y).start()
 
     @pl.loop(0, n_outer)
     def _(n):
+        rs_core(turn(n), y).start()
+
+    def send_other(n):
         d = turn(n)
         rs_core(d, 1 - y).wait_recv()
         for h in range(2):
             send_y[d, h] = chip_sum(d, 1 - y, h)
             rs_y(d, h).start()
+
+    send_other(0)
+    for y_of in range(INNER):
+        last_core(y_of).wait_recv()
+
+    @pl.loop(0, n_outer - 1)
+    def _(n):
+        d = turn(n)
+        for y_of in range(INNER):
+            last_send_z[d, y_of] = last_sum(d, y_of)
+        last_z(d).start()
+
+    @pl.loop(1, n_outer)
+    def _(n):
+        send_other(n)
 
     @pl.loop(0, n_outer - 1)
     def _(n):
@@ -416,6 +471,15 @@
             send_z[d, h] = chip_sum(d, y, h) + got_y[d, h]
             rs_z(d, h).start()
 
+    last_own, last_other = last_sum(z, y), last_sum(z, 1 - y)
+    for k in range(1, n_outer):
+        z_from = fwd(k)
+        got = last_got_z.at[z_from]
+        send(got, got, all_sent, last_z_recv.at[z_from], dp, 1 - v).wait_recv()
+        last_own = last_own + last_got_z[z_from, y]
+        last_other = last_other + last_got_z[z_from, 1 - y]
+    last_send_y[...] = last_other
+    last_y.start()
     rs_core(z, y).wait_recv()
     row_halves = []
     for h in range(2):
@@ -427,7 +491,8 @@
             send(got, got, all_sent, rs_z_recv.at[z_from, h], dp, 1 - v).wait_recv()
             row_half = row_half + got_z[z_from, h]
         row_halves.append(row_half)
-    rows8 = jnp.concatenate(row_halves, axis=1)
+    last_y.wait_recv()
+    rows8 = jnp.concatenate([*row_halves, last_own + last_got_y[...]], axis=1)
     low, high = rows8[:own_rows], rows8[own_rows:]
     grad_near = jnp.where(v == 0, low, high)
     grad_far = jnp.where(v == 0, high, low)
@@ -524,6 +589,7 @@
     own_rows, width = head.shape[1], head.shape[2]
     n_outer = n_dp // (CORES * INNER)
     pair = 2 * own_rows
+    quarter = half // 4
     block = n_dp * pair
     vmem = pl.BlockSpec(memory_space=pltpu.VMEM)
     anywhere = pl.BlockSpec(memory_space=pltpu.HBM)
@@ -548,11 +614,16 @@
             pltpu.VMEM((INNER, masked // 2, block), F32),
             pltpu.VMEM((INNER, masked // 2, block), F32),
             pltpu.VMEM((n_dp, pair, half), F32),
-            pltpu.VMEM((n_outer, INNER, pair, half), F32),
-            pltpu.VMEM((n_outer, 2, pair, half // 2), F32),
-            pltpu.VMEM((n_outer, 2, pair, half // 2), F32),
-            pltpu.VMEM((n_outer, 2, pair, half // 2), F32),
-            pltpu.VMEM((n_outer, 2, pair, half // 2), F32),
+            pltpu.VMEM((n_outer, INNER, pair, half - quarter), F32),
+            pltpu.VMEM((INNER, n_outer, pair, quarter), F32),
+            pltpu.VMEM((n_outer, INNER, pair, quarter), F32),
+            pltpu.VMEM((n_outer, INNER, pair, quarter), F32),
+            pltpu.VMEM((pair, quarter), F32),
+            pltpu.VMEM((pair, quarter), F32),
+            pltpu.VMEM((n_outer, 2, pair, (half - quarter) // 2), F32),
+            pltpu.VMEM((n_outer, 2, pair, (half - quarter) // 2), F32),
+            pltpu.VMEM((n_outer, 2, pair, (half - quarter) // 2), F32),
+            pltpu.VMEM((n_outer, 2, pair, (half - quarter) // 2), F32),
             pltpu.VMEM((own_rows, half), F32),
             pltpu.VMEM((own_rows, half), F32),
             pltpu.VMEM((2, own_rows, half), F32),
@@ -569,12 +640,15 @@
             dma((6,)),
             dma,
             dma,
-            dma((n_outer,)),
+            dma((n_outer, 2)),
             dma((n_outer,)),
             dma((INNER,)),
             dma((INNER, max(seqs // 2, 1))),
             dma((INNER,)),
             dma((n_outer, INNER)),
+            dma((INNER,)),
+            dma((n_outer,)),
+            dma,
             dma((n_outer, 2)),
             dma((n_outer, 2)),
             dma,
@@ -662,8 +736,8 @@
     power_of_two = own_rows & (own_rows - 1) == 0
     n_outer = n_dp // (CORES * INNER)
     power_of_two = power_of_two and n_outer & (n_outer - 1) == 0
-    masked = args[1].shape[1]
-    power_of_two = power_of_two and masked % 16 == 0
+    masked, width = args[1].shape[1], args[4].shape[2]
+    power_of_two = power_of_two and masked % 16 == 0 and width % 2048 == 0
     return n_vocab == 2 and n_dp % (CORES * INNER) == 0 and power_of_two
 
 

time: 38.9 us -> 38.3 us (0.985)
  Pallas kernels: 38.1 us -> 37.6 us
    pallas_call x1, Pallas kernels: 37.4 us -> 36.8 us  [fused_step(): pl.pallas_call(functools.partial(step_kernel, n_dp), out_shape=(jax.Shape...]
where the time goes in v5:
time: 38.3 us; the launch traced here: 38.2 us
  Pallas kernels  37.6 us (98%)
  between operations  0.64 us (2%)
    pallas_call x1, Pallas kernels, fused_step(): pl.pallas_call(functools.partial(step_kernel, n_dp), out_shape=(jax.Shape...  36.8 us

profile of v5, /device:TPU:0, one launch (start us, length us, event | category | flops | bytes accessed | tf_op | source)
XLA Modules:
  0.0 38.2 jit_solution(15274491469052251038)
XLA Ops:
  0.6 36.8 %fused_step.1 = (f32[5,80]{1,0:T(8,128)S(1)}, f32[1,4,4096]{2,1,0:T(4,128)S(1)}, f32[1,4,4096]{2,1,0:T(4,128)S(1)}, f32[1,4,4096]{2,1,0:T(4,128)S(1)}) custom-call(bf16[5,512,2048]{2,1,0:T(8,128)(2,1)} %hidden_ref.1, s32[5,80]{1,0:T(8,128)} %positions_hbm.1, s32[5,80]{1,0:T(8,128)} %labels_hbm.1, f32[5,80]{1,0:T(8,128)} %lse_hbm.1, f32[1,4,4096]{2,1,0:T(4,128)} %head_hbm.1, ...), custom_call_target="tpu_custom_call" | custom-call | tf_op jit(solution)/shard_map/fused_step/pallas_call | solution.py:602
  37.5 0.7 %store_results.1 = (f32[5,80]{1,0:T(8,128)}, f32[1,4,4096]{2,1,0:T(4,128)}, f32[1,4,4096]{2,1,0:T(4,128)}, f32[1,4,4096]{2,1,0:T(4,128)}) custom-call(f32[5,80]{1,0:T(8,128)S(1)} %get-tuple-element.8.refs_0_, f32[1,4,4096]{2,1,0:T(4,128)S(1)} %get-tuple-element.9.refs_1_, f32[1,4,4096]{2,1,0:T(4,128)S(1)} %get-tuple-element.10.refs_2_, ...), custom_call_target="tpu_custom_call" | custom-call | tf_op jit(solution)/shard_map/store_results/pallas_call | solution.py:664

commit v6 on v5

--- a/solution.py
+++ b/solution.py
@@ -17,6 +17,7 @@
 MESH = pl.DeviceIdType.MESH
 CORES = 2
 INNER = 2
+PARTS = 1
 F32 = jnp.float32
 BF16 = jnp.bfloat16
 
@@ -241,8 +242,8 @@
         core_copy(z_from, y).start()
 
     near_first(lambda z_from: pass_piece(z_from, v))
+    picks(late, seqs)
     near_first(pass_on)
-    picks(late, seqs)
     load_labels.wait()
     load_lse.wait()
 
@@ -325,7 +326,6 @@
     sent.append((1, n_outer, lambda k: (outer_copy(z, 0), outer_copy(z, 1))))
     sent.append((0, n_outer, lambda k: (inner_copy(k, 0), inner_copy(k, 1), core_copy(k, 0), core_copy(k, 1))))
 
-    grads[...] = jnp.zeros_like(grads)
     row = lax.broadcasted_iota(jnp.int32, (block, masked), 0)
     shift = own_rows.bit_length() - 1
     slot = lax.shift_right_logical(row, shift + 1)
@@ -339,28 +339,35 @@
         + (row & (own_rows - 1))
     )
 
-    def finish_seq(seq, scores):
+    def logit_grad(seq, scores):
         rest = lse_ref[pl.ds(seq, 1), :]
         top = jnp.maximum(jnp.max(scores, axis=0, keepdims=True), rest)
-        total = jnp.exp(rest - top) + jnp.sum(jnp.exp(scores - top), axis=0, keepdims=True)
-        row_lse = top + jnp.log(total)
+        exps = jnp.exp(scores - top)
+        total = jnp.exp(rest - top) + jnp.sum(exps, axis=0, keepdims=True)
         hits = row_id == labels_ref[pl.ds(seq, 1), :]
         target = jnp.sum(jnp.where(hits, scores, 0.0), axis=0, keepdims=True)
-        losses_ref[pl.ds(seq, 1), :] = row_lse - target
-        logit_grad = (jnp.exp(scores - row_lse) - jnp.where(hits, 1.0, 0.0)).astype(BF16)
-        grads[...] += lax.dot_general(
-            logit_grad, picked[seq], (((1,), (0,)), ((), ())), preferred_element_type=F32
+        losses_ref[pl.ds(seq, 1), :] = top + jnp.log(total) - target
+        return exps * (1.0 / total) - jnp.where(hits, 1.0, 0.0)
+
+    def add_grads(seq, count, logits):
+        new = lax.dot_general(
+            logits.astype(BF16),
+            picked[pl.ds(seq, count)].reshape(count * masked, half),
+            (((1,), (0,)), ((), ())),
+            preferred_element_type=F32,
         ).reshape(n_dp, 2 * own_rows, half)
-
-    @pl.loop(0, pairs)
-    def _(m):
+        grads[...] = new if seq == 0 else grads[...] + new
+
+    for m in range(pairs):
         turned = []
         for y_of in range(INNER):
             score_copy(y_of, m).wait_recv()
             turned.append(jnp.transpose(score_own[y_of, m] + score_other[y_of, m]))
+        logits = []
         for n in range(2):
             rows = slice(n * side, (n + 1) * side)
-            finish_seq(2 * m + n, jnp.concatenate([t[rows] for t in turned], axis=0))
+            logits.append(logit_grad(2 * m + n, jnp.concatenate([t[rows] for t in turned], axis=0)))
+        add_grads(2 * m, 2, jnp.concatenate(logits, axis=1))
 
     if odd:
         turned = []
@@ -368,14 +375,14 @@
             tail_copy(y_of).wait_recv()
             turned.append(jnp.transpose(tail_own[y_of] + tail_other[y_of]))
         sides = [jnp.concatenate([t[n * side : (n + 1) * side] for t in turned], axis=0) for n in range(2)]
-        finish_seq(seqs - 1, jnp.concatenate(sides, axis=1))
+        add_grads(seqs - 1, 1, logit_grad(seqs - 1, jnp.concatenate(sides, axis=1)))
 
     for copy in state_copies:
         copy.start()
 
     quarter = half // 4
     main = half - quarter
-    part = main // 2
+    part = main // PARTS
 
     def turn(n):
         down = n_outer - 1 - n
@@ -424,8 +431,8 @@
         return grads[spot(d, y_of, c), :, pl.ds(main, quarter)] + last_got_core[y_of, d]
 
     last_y = send(last_send_y, last_got_y, all_sent, last_y_recv, other_y, v)
-    sent.append((0, n_outer, lambda k: (rs_core(k, 0), rs_core(k, 1), rs_y(k, 0), rs_y(k, 1))))
-    sent.append((1, n_outer, lambda k: (rs_z(z, 0), rs_z(z, 1), last_z(z))))
+    sent.append((0, n_outer, lambda k: [rs_core(k, 0), rs_core(k, 1)] + [rs_y(k, h) for h in range(PARTS)]))
+    sent.append((1, n_outer, lambda k: [last_z(z)] + [rs_z(z, h) for h in range(PARTS)]))
     sent.append((0, 1, lambda k: (last_core(0), last_core(1), last_y)))
 
     rs_core(turn(0), 1 - y).start()
@@ -443,7 +450,7 @@
     def send_other(n):
         d = turn(n)
         rs_core(d, 1 - y).wait_recv()
-        for h in range(2):
+        for h in range(PARTS):
             send_y[d, h] = chip_sum(d, 1 - y, h)
             rs_y(d, h).start()
 
@@ -466,7 +473,7 @@
     def _(n):
         d = turn(n)
         rs_core(d, y).wait_recv()
-        for h in range(2):
+        for h in range(PARTS):
             rs_y(d, h).wait_recv()
             send_z[d, h] = chip_sum(d, y, h) + got_y[d, h]
             rs_z(d, h).start()
@@ -482,7 +489,7 @@
     last_y.start()
     rs_core(z, y).wait_recv()
     row_halves = []
-    for h in range(2):
+    for h in range(PARTS):
         rs_y(z, h).wait_recv()
         row_half = chip_sum(z, y, h) + got_y[z, h]
         for k in range(1, n_outer):
@@ -620,10 +627,10 @@
             pltpu.VMEM((n_outer, INNER, pair, quarter), F32),
             pltpu.VMEM((pair, quarter), F32),
             pltpu.VMEM((pair, quarter), F32),
-            pltpu.VMEM((n_outer, 2, pair, (half - quarter) // 2), F32),
-            pltpu.VMEM((n_outer, 2, pair, (half - quarter) // 2), F32),
-            pltpu.VMEM((n_outer, 2, pair, (half - quarter) // 2), F32),
-            pltpu.VMEM((n_outer, 2, pair, (half - quarter) // 2), F32),
+            pltpu.VMEM((n_outer, PARTS, pair, (half - quarter) // PARTS), F32),
+            pltpu.VMEM((n_outer, PARTS, pair, (half - quarter) // PARTS), F32),
+            pltpu.VMEM((n_outer, PARTS, pair, (half - quarter) // PARTS), F32),
+            pltpu.VMEM((n_outer, PARTS, pair, (half - quarter) // PARTS), F32),
             pltpu.VMEM((own_rows, half), F32),
             pltpu.VMEM((own_rows, half), F32),
             pltpu.VMEM((2, own_rows, half), F32),
@@ -649,8 +656,8 @@
             dma((INNER,)),
             dma((n_outer,)),
             dma,
-            dma((n_outer, 2)),
-            dma((n_outer, 2)),
+            dma((n_outer, PARTS)),
+            dma((n_outer, PARTS)),
             dma,
             dma,
             dma((2,)),

time: 38.3 us -> 38 us (level)
  Pallas kernels: 37.6 us -> 37.2 us
where the time goes in v6:
time: 38 us; the launch traced here: 37.8 us
  Pallas kernels  37.2 us (98%)
  between operations  0.64 us (2%)
    pallas_call x1, Pallas kernels, fused_step(): pl.pallas_call(functools.partial(step_kernel, n_dp), out_shape=(jax.Shape...  36.5 us

profile of v6, /device:TPU:0, one launch (start us, length us, event | category | flops | bytes accessed | tf_op | source)
XLA Modules:
  0.0 37.8 jit_solution(10345597298669995003)
XLA Ops:
  0.6 36.5 %fused_step.1 = (f32[5,80]{1,0:T(8,128)S(1)}, f32[1,4,4096]{2,1,0:T(4,128)S(1)}, f32[1,4,4096]{2,1,0:T(4,128)S(1)}, f32[1,4,4096]{2,1,0:T(4,128)S(1)}) custom-call(bf16[5,512,2048]{2,1,0:T(8,128)(2,1)} %hidden_ref.1, s32[5,80]{1,0:T(8,128)} %positions_hbm.1, s32[5,80]{1,0:T(8,128)} %labels_hbm.1, f32[5,80]{1,0:T(8,128)} %lse_hbm.1, f32[1,4,4096]{2,1,0:T(4,128)} %head_hbm.1, ...), custom_call_target="tpu_custom_call" | custom-call | tf_op jit(solution)/shard_map/fused_step/pallas_call | solution.py:609
  37.1 0.7 %store_results.1 = (f32[5,80]{1,0:T(8,128)}, f32[1,4,4096]{2,1,0:T(4,128)}, f32[1,4,4096]{2,1,0:T(4,128)}, f32[1,4,4096]{2,1,0:T(4,128)}) custom-call(f32[5,80]{1,0:T(8,128)S(1)} %get-tuple-element.8.refs_0_, f32[1,4,4096]{2,1,0:T(4,128)S(1)} %get-tuple-element.9.refs_1_, f32[1,4,4096]{2,1,0:T(4,128)S(1)} %get-tuple-element.10.refs_2_, ...), custom_call_target="tpu_custom_call" | custom-call | tf_op jit(solution)/shard_map/store_results/pallas_call | solution.py:671
